TPU v7x, 32 devices: a whole 2x2x4 slice. The times are simulated.
32 devices in a mesh: dp: 8 (over z, y), seq: 4 (over x, core).
Axes of the slice: x: 2, y: 2, z: 4, core: 2. Of those that a mesh axis runs over, the one named last changes fastest.
Arguments:
- tokens: bfloat16 [8, 1024, 1024], P('dp', 'seq'), may hold values from -6 to 6
- segments: int32 [8, 1024], P('dp'), may hold values from 0 to 1023, as said below
- valid_mask: int32 [8, 1024], P('dp'), may hold values from 0 to 1, as said below
- attention_gain: float32 [1024], P('dp'), may hold values from 0.25 to 1.75
- query_weight: float32 [1024, 1024], P('dp'), may hold values from -0.1875 to 0.1875
- key_weight: float32 [1024, 512], P('dp'), may hold values from -0.1875 to 0.1875
- value_weight: float32 [1024, 512], P('dp'), may hold values from -0.1875 to 0.1875
- query_gain: float32 [64], replicated, may hold values from 0.25 to 1.75
- key_gain: float32 [64], replicated, may hold values from 0.25 to 1.75
- output_weight: float32 [1024, 1024], P('dp'), may hold values from -0.5 to 0.5
- feedforward_gain: float32 [1024], P('dp'), may hold values from 0.25 to 1.75
- gate_weight: float32 [1024, 4608], P('dp'), may hold values from -0.1875 to 0.1875
- up_weight: float32 [1024, 4608], P('dp'), may hold values from -0.1875 to 0.1875
- down_weight: float32 [4608, 1024], P('dp'), may hold values from -0.09375 to 0.09375
- cotangent: bfloat16 [8, 1024, 1024], P('dp', 'seq'), may hold values from -6 to 6
Outputs:
- layer_out: bfloat16 [8, 1024, 1024], P('dp', 'seq')
- token_grad: bfloat16 [8, 1024, 1024], P('dp', 'seq')
- attention_gain_grad: float32 [1024], P(('dp', 'seq'))
- query_weight_grad: float32 [1024, 1024], P(('dp', 'seq'))
- key_weight_grad: float32 [1024, 512], P(('dp', 'seq'))
- value_weight_grad: float32 [1024, 512], P(('dp', 'seq'))
- query_gain_grad: float32 [64], replicated
- key_gain_grad: float32 [64], replicated
- output_weight_grad: float32 [1024, 1024], P(('dp', 'seq'))
- feedforward_gain_grad: float32 [1024], P(('dp', 'seq'))
- gate_weight_grad: float32 [1024, 4608], P(('dp', 'seq'))
- up_weight_grad: float32 [1024, 4608], P(('dp', 'seq'))
- down_weight_grad: float32 [4608, 1024], P(('dp', 'seq'))
Inputs may be any that keep to these rules, and one draw needn't show every extreme that they name: `segments`: document numbers start at 0 in each row and never fall; the row's last document is numbered 1024 - 1; every document but one has at most 128 tokens, and one document of exactly 512 tokens lies wholly among the row's valid tokens. `valid_mask`: each row is 1 on its first 1024 - k positions and 0 after them, for some k from 0 to 128.
All inputs are finite; a program needn't handle non-finite values.
Results may differ from a plain program's by a relative error of at most 0.017.
Values may be sent and summed in bfloat16 or wider, within the bound.
No kernel may reach another device: no remote copies, remote signals or barrier semaphores. Data moves between devices by JAX's collectives and lax.ppermute only.
A program may use at most 192 MiB of HBM per device.

v0:
```python
import math

import jax
import jax.numpy as jnp
from jax import lax
from jax.sharding import PartitionSpec as P

EPS = 1e-05
ROPE_BASE = 1000000.0
NEG_FILL = -1e30


def rms_stats(values):
    factor = lax.rsqrt(jnp.mean(values * values, axis=-1, keepdims=True) + EPS)
    return (values * factor, factor)


def rms_back(grad_unit, unit_values, factor):
    return factor * (
        grad_unit - unit_values * jnp.mean(grad_unit * unit_values, axis=-1, keepdims=True)
    )


def doc_positions(segment_row):
    length = segment_row.shape[0]
    places = jnp.arange(length, dtype=jnp.int32)
    change = jnp.concatenate([jnp.ones((1,), dtype=jnp.bool_), segment_row[1:] != segment_row[:-1]])
    starts = lax.cummax(jnp.where(change, places, jnp.zeros_like(places)), axis=0)
    return places - starts


def rope_tables(positions, half_dim):
    frequency = ROPE_BASE ** (-jnp.arange(half_dim, dtype=jnp.float32) / half_dim)
    angles = positions.astype(jnp.float32)[:, None] * frequency[None, :]
    return (jnp.cos(angles), jnp.sin(angles))


def rotate(values, cos_table, sin_table):
    half_dim = values.shape[-1] // 2
    first_half = values[..., :half_dim]
    second_half = values[..., half_dim:]
    cos_wide = cos_table[:, None, :]
    sin_wide = sin_table[:, None, :]
    return jnp.concatenate(
        [
            first_half * cos_wide - second_half * sin_wide,
            second_half * cos_wide + first_half * sin_wide,
        ],
        axis=-1,
    )


def unrotate(grad_values, cos_table, sin_table):
    half_dim = grad_values.shape[-1] // 2
    first_half = grad_values[..., :half_dim]
    second_half = grad_values[..., half_dim:]
    cos_wide = cos_table[:, None, :]
    sin_wide = sin_table[:, None, :]
    return jnp.concatenate(
        [
            first_half * cos_wide + second_half * sin_wide,
            second_half * cos_wide - first_half * sin_wide,
        ],
        axis=-1,
    )


def block_mask(segment_row, valid_row, first_row, block_rows):
    length = segment_row.shape[0]
    columns = jnp.arange(length, dtype=jnp.int32)
    rows_here = first_row + jnp.arange(block_rows, dtype=jnp.int32)
    segment_here = lax.dynamic_slice_in_dim(segment_row, first_row, block_rows, 0)
    return (columns[None, :] <= rows_here[:, None]) & (
        segment_here[:, None] == segment_row[None, :]
    ) & (valid_row[None, :] > 0) | (columns[None, :] == rows_here[:, None])


def block_scores(query_block, keys_all, allowed, score_scale):
    scores = (
        jnp.einsum("qgrd,kgd->grqk", query_block, keys_all, preferred_element_type=jnp.float32)
        * score_scale
    )
    return jnp.where(allowed[None, None], scores, NEG_FILL)


def attention_forward(queries, keys_all, values_all, segment_row, valid_row, score_scale):
    block_count = queries.shape[0]
    block_rows = queries.shape[1]

    def one_block(block_items):
        query_block, block_index = block_items
        allowed = block_mask(segment_row, valid_row, block_index * block_rows, block_rows)
        scores = block_scores(query_block, keys_all, allowed, score_scale)
        largest = jnp.max(scores, axis=-1, keepdims=True)
        weights_exp = jnp.exp(scores - largest)
        totals = jnp.sum(weights_exp, axis=-1, keepdims=True)
        shares = (weights_exp / totals).astype(jnp.bfloat16)
        mixed_block = jnp.einsum(
            "grqk,kgd->qgrd", shares, values_all, preferred_element_type=jnp.float32
        )
        return (mixed_block.astype(jnp.bfloat16), (largest + jnp.log(totals))[..., 0])

    return lax.map(one_block, (queries, jnp.arange(block_count, dtype=jnp.int32)))


def attention_backward(
    queries, keys_all, values_all, grad_out, log_totals, segment_row, valid_row, score_scale
):
    block_count = queries.shape[0]
    block_rows = queries.shape[1]

    def one_block(running, block_items):
        key_sum, value_sum = running
        query_block, grad_block, log_block, block_index = block_items
        allowed = block_mask(segment_row, valid_row, block_index * block_rows, block_rows)
        scores = block_scores(query_block, keys_all, allowed, score_scale)
        shares = jnp.exp(scores - log_block[..., None])
        grad_shares = jnp.einsum(
            "qgrd,kgd->grqk", grad_block, values_all, preferred_element_type=jnp.float32
        )
        centre = jnp.sum(shares * grad_shares, axis=-1, keepdims=True)
        grad_scores = (shares * (grad_shares - centre)).astype(jnp.bfloat16)
        grad_query = (
            jnp.einsum("grqk,kgd->qgrd", grad_scores, keys_all, preferred_element_type=jnp.float32)
            * score_scale
        )
        key_sum = (
            key_sum
            + jnp.einsum(
                "grqk,qgrd->kgd", grad_scores, query_block, preferred_element_type=jnp.float32
            )
            * score_scale
        )
        value_sum = value_sum + jnp.einsum(
            "grqk,qgrd->kgd",
            shares.astype(jnp.bfloat16),
            grad_block,
            preferred_element_type=jnp.float32,
        )
        return ((key_sum, value_sum), grad_query.astype(jnp.bfloat16))

    zero_keys = jnp.zeros(keys_all.shape, jnp.float32)
    zero_values = jnp.zeros(values_all.shape, jnp.float32)
    sums_out, query_grad = lax.scan(
        one_block,
        (zero_keys, zero_values),
        (queries, grad_out, log_totals, jnp.arange(block_count, dtype=jnp.int32)),
    )
    return (sums_out[0], sums_out[1], query_grad)


def local(
    tokens,
    segments,
    valid_mask,
    attention_gain,
    query_weight,
    key_weight,
    value_weight,
    query_gain,
    key_gain,
    output_weight,
    feedforward_gain,
    gate_weight,
    up_weight,
    down_weight,
    cotangent,
):
    seq_count = lax.axis_size("seq")
    seq_place = lax.axis_index("seq")
    local_rows = tokens.shape[1]
    row_length = segments.shape[1]
    head_dim = query_gain.shape[0]
    query_width = query_weight.shape[1]
    key_width = key_weight.shape[1]
    heads_here = query_width // seq_count // head_dim
    groups_here = key_width // seq_count // head_dim
    group_size = heads_here // groups_here
    block_rows = min(512, row_length)
    block_count = row_length // block_rows
    score_scale = 1.0 / math.sqrt(head_dim)
    segment_row = segments[0]
    valid_row = valid_mask[0]
    attention_set = (
        lax.all_gather(attention_gain.astype(jnp.bfloat16), "dp", axis=0, tiled=True),
        lax.all_gather(query_weight.astype(jnp.bfloat16), "dp", axis=0, tiled=True),
        lax.all_gather(key_weight.astype(jnp.bfloat16), "dp", axis=0, tiled=True),
        lax.all_gather(value_weight.astype(jnp.bfloat16), "dp", axis=0, tiled=True),
        lax.all_gather(output_weight.astype(jnp.bfloat16), "dp", axis=0, tiled=True),
    )
    feed_set = (
        lax.all_gather(feedforward_gain.astype(jnp.bfloat16), "dp", axis=0, tiled=True),
        lax.all_gather(gate_weight.astype(jnp.bfloat16), "dp", axis=0, tiled=True),
        lax.all_gather(up_weight.astype(jnp.bfloat16), "dp", axis=0, tiled=True),
        lax.all_gather(down_weight.astype(jnp.bfloat16), "dp", axis=0, tiled=True),
    )
    positions = lax.dynamic_slice_in_dim(
        doc_positions(segment_row), seq_place * local_rows, local_rows, 0
    )
    cos_table, sin_table = rope_tables(positions, head_dim // 2)
    inputs = tokens[0].astype(jnp.float32)
    gain_one = attention_set[0].astype(jnp.float32)
    unit_one, factor_one = rms_stats(inputs)
    normed_one = (unit_one * gain_one).astype(jnp.bfloat16)
    query_raw = jnp.dot(normed_one, attention_set[1], preferred_element_type=jnp.float32)
    key_raw = jnp.dot(normed_one, attention_set[2], preferred_element_type=jnp.float32)
    value_raw = jnp.dot(normed_one, attention_set[3], preferred_element_type=jnp.float32)
    query_unit, query_factor = rms_stats(query_raw.reshape(local_rows, -1, head_dim))
    key_unit, key_factor = rms_stats(key_raw.reshape(local_rows, -1, head_dim))
    query_send = rotate(query_unit * query_gain, cos_table, sin_table).astype(jnp.bfloat16)
    key_send = rotate(key_unit * key_gain, cos_table, sin_table).astype(jnp.bfloat16)
    value_send = value_raw.astype(jnp.bfloat16)
    query_heads, key_heads, value_heads = (
        lax.all_to_all(
            query_send.reshape(local_rows, seq_count, -1),
            "seq",
            split_axis=1,
            concat_axis=0,
            tiled=True,
        ),
        lax.all_to_all(
            key_send.reshape(local_rows, seq_count, -1),
            "seq",
            split_axis=1,
            concat_axis=0,
            tiled=True,
        ),
        lax.all_to_all(
            value_send.reshape(local_rows, seq_count, -1),
            "seq",
            split_axis=1,
            concat_axis=0,
            tiled=True,
        ),
    )
    query_blocks = query_heads.reshape(block_count, block_rows, groups_here, group_size, head_dim)
    keys_all = key_heads.reshape(row_length, groups_here, head_dim)
    values_all = value_heads.reshape(row_length, groups_here, head_dim)
    mixed_blocks, log_totals = attention_forward(
        query_blocks, keys_all, values_all, segment_row, valid_row, score_scale
    )
    mixed_local = lax.all_to_all(
        mixed_blocks.reshape(row_length, 1, -1), "seq", split_axis=0, concat_axis=1, tiled=True
    ).reshape(local_rows, query_width)
    after_attention = inputs + jnp.dot(
        mixed_local, attention_set[4], preferred_element_type=jnp.float32
    )
    gain_two = feed_set[0].astype(jnp.float32)
    unit_two, factor_two = rms_stats(after_attention)
    normed_two = (unit_two * gain_two).astype(jnp.bfloat16)
    grad_rows = cotangent[0]
    gate_use = feed_set[1]
    up_use = feed_set[2]
    down_use = feed_set[3]
    gate_value = jnp.dot(normed_two, gate_use, preferred_element_type=jnp.float32)
    up_value = jnp.dot(normed_two, up_use, preferred_element_type=jnp.float32)
    sigmoid_gate = jax.nn.sigmoid(gate_value)
    silu_gate = gate_value * sigmoid_gate
    hidden = (silu_gate * up_value).astype(jnp.bfloat16)
    down_term = jnp.dot(hidden, down_use, preferred_element_type=jnp.float32)
    layer_out = (after_attention + down_term).astype(jnp.bfloat16)
    feed_back = (
        lax.all_gather(feedforward_gain.astype(jnp.bfloat16), "dp", axis=0, tiled=True),
        lax.all_gather(gate_weight.astype(jnp.bfloat16), "dp", axis=0, tiled=True),
        lax.all_gather(up_weight.astype(jnp.bfloat16), "dp", axis=0, tiled=True),
        lax.all_gather(down_weight.astype(jnp.bfloat16), "dp", axis=0, tiled=True),
    )
    back_gate = feed_back[1]
    back_up = feed_back[2]
    back_down = feed_back[3]
    down_grad = jnp.einsum("tf,td->fd", hidden, grad_rows, preferred_element_type=jnp.float32)
    grad_hidden = jnp.einsum("td,fd->tf", grad_rows, back_down, preferred_element_type=jnp.float32)
    grad_gate = (
        grad_hidden * up_value * sigmoid_gate * (1.0 + gate_value * (1.0 - sigmoid_gate))
    ).astype(jnp.bfloat16)
    grad_up = (grad_hidden * silu_gate).astype(jnp.bfloat16)
    gate_grad = jnp.einsum("td,tf->df", normed_two, grad_gate, preferred_element_type=jnp.float32)
    up_grad = jnp.einsum("td,tf->df", normed_two, grad_up, preferred_element_type=jnp.float32)
    grad_normed_term = jnp.einsum(
        "tf,df->td", grad_gate, back_gate, preferred_element_type=jnp.float32
    ) + jnp.einsum("tf,df->td", grad_up, back_up, preferred_element_type=jnp.float32)
    feed_gain_grad = jnp.sum(grad_normed_term * unit_two, axis=0)
    grad_after = cotangent[0].astype(jnp.float32) + rms_back(
        grad_normed_term * gain_two, unit_two, factor_two
    )
    feed_rowsums = (
        lax.psum_scatter(gate_grad, "dp", scatter_dimension=0, tiled=True),
        lax.psum_scatter(up_grad, "dp", scatter_dimension=0, tiled=True),
        lax.psum_scatter(down_grad, "dp", scatter_dimension=0, tiled=True),
    )
    feed_sums = (
        lax.psum_scatter(
            feed_rowsums[0].astype(jnp.bfloat16), "seq", scatter_dimension=0, tiled=True
        ).astype(jnp.float32),
        lax.psum_scatter(
            feed_rowsums[1].astype(jnp.bfloat16), "seq", scatter_dimension=0, tiled=True
        ).astype(jnp.float32),
        lax.psum_scatter(
            feed_rowsums[2].astype(jnp.bfloat16), "seq", scatter_dimension=0, tiled=True
        ).astype(jnp.float32),
    )
    attention_back = (
        lax.all_gather(attention_gain.astype(jnp.bfloat16), "dp", axis=0, tiled=True),
        lax.all_gather(query_weight.astype(jnp.bfloat16), "dp", axis=0, tiled=True),
        lax.all_gather(key_weight.astype(jnp.bfloat16), "dp", axis=0, tiled=True),
        lax.all_gather(value_weight.astype(jnp.bfloat16), "dp", axis=0, tiled=True),
        lax.all_gather(output_weight.astype(jnp.bfloat16), "dp", axis=0, tiled=True),
    )
    grad_branch = grad_after.astype(jnp.bfloat16)
    output_grad = jnp.einsum(
        "tf,td->fd", mixed_local, grad_branch, preferred_element_type=jnp.float32
    )
    grad_mixed = jnp.einsum(
        "td,fd->tf", grad_branch, attention_back[4], preferred_element_type=jnp.float32
    ).astype(jnp.bfloat16)
    grad_heads = lax.all_to_all(
        grad_mixed.reshape(local_rows, seq_count, -1),
        "seq",
        split_axis=1,
        concat_axis=0,
        tiled=True,
    )
    grad_blocks = grad_heads.reshape(block_count, block_rows, groups_here, group_size, head_dim)
    key_sum, value_sum, query_grad = attention_backward(
        query_blocks,
        keys_all,
        values_all,
        grad_blocks,
        log_totals,
        segment_row,
        valid_row,
        score_scale,
    )
    query_back, key_back, value_back = (
        lax.all_to_all(
            query_grad.reshape(row_length, 1, -1), "seq", split_axis=0, concat_axis=1, tiled=True
        ),
        lax.all_to_all(
            key_sum.astype(jnp.bfloat16).reshape(row_length, 1, -1),
            "seq",
            split_axis=0,
            concat_axis=1,
            tiled=True,
        ),
        lax.all_to_all(
            value_sum.astype(jnp.bfloat16).reshape(row_length, 1, -1),
            "seq",
            split_axis=0,
            concat_axis=1,
            tiled=True,
        ),
    )
    query_turned = unrotate(
        query_back.reshape(local_rows, -1, head_dim).astype(jnp.float32), cos_table, sin_table
    )
    key_turned = unrotate(
        key_back.reshape(local_rows, -1, head_dim).astype(jnp.float32), cos_table, sin_table
    )
    query_gain_term = jnp.sum(query_turned * query_unit, axis=(0, 1))
    key_gain_term = jnp.sum(key_turned * key_unit, axis=(0, 1))
    query_raw_grad = (
        rms_back(query_turned * query_gain, query_unit, query_factor)
        .astype(jnp.bfloat16)
        .reshape(local_rows, query_width)
    )
    key_raw_grad = (
        rms_back(key_turned * key_gain, key_unit, key_factor)
        .astype(jnp.bfloat16)
        .reshape(local_rows, key_width)
    )
    value_raw_grad = value_back.reshape(local_rows, key_width)
    query_w_grad = jnp.einsum(
        "td,tf->df", normed_one, query_raw_grad, preferred_element_type=jnp.float32
    )
    key_w_grad = jnp.einsum(
        "td,tf->df", normed_one, key_raw_grad, preferred_element_type=jnp.float32
    )
    value_w_grad = jnp.einsum(
        "td,tf->df", normed_one, value_raw_grad, preferred_element_type=jnp.float32
    )
    grad_normed_one = jnp.einsum(
        "tf,df->td", query_raw_grad, attention_back[1], preferred_element_type=jnp.float32
    )
    grad_normed_one = grad_normed_one + jnp.einsum(
        "tf,df->td", key_raw_grad, attention_back[2], preferred_element_type=jnp.float32
    )
    grad_normed_one = grad_normed_one + jnp.einsum(
        "tf,df->td", value_raw_grad, attention_back[3], preferred_element_type=jnp.float32
    )
    attention_gain_term = jnp.sum(grad_normed_one * unit_one, axis=0)
    token_grad = (grad_after + rms_back(grad_normed_one * gain_one, unit_one, factor_one)).astype(
        jnp.bfloat16
    )
    gain_sums = lax.psum((query_gain_term, key_gain_term), ("dp", "seq"))
    over_dp = (
        lax.psum_scatter(attention_gain_term, "dp", scatter_dimension=0, tiled=True),
        lax.psum_scatter(query_w_grad, "dp", scatter_dimension=0, tiled=True),
        lax.psum_scatter(key_w_grad, "dp", scatter_dimension=0, tiled=True),
        lax.psum_scatter(value_w_grad, "dp", scatter_dimension=0, tiled=True),
        lax.psum_scatter(output_grad, "dp", scatter_dimension=0, tiled=True),
        lax.psum_scatter(feed_gain_grad, "dp", scatter_dimension=0, tiled=True),
    )
    attention_sums = (
        lax.psum_scatter(
            over_dp[0].astype(jnp.bfloat16), "seq", scatter_dimension=0, tiled=True
        ).astype(jnp.float32),
        lax.psum_scatter(
            over_dp[1].astype(jnp.bfloat16), "seq", scatter_dimension=0, tiled=True
        ).astype(jnp.float32),
        lax.psum_scatter(
            over_dp[2].astype(jnp.bfloat16), "seq", scatter_dimension=0, tiled=True
        ).astype(jnp.float32),
        lax.psum_scatter(
            over_dp[3].astype(jnp.bfloat16), "seq", scatter_dimension=0, tiled=True
        ).astype(jnp.float32),
        lax.psum_scatter(
            over_dp[4].astype(jnp.bfloat16), "seq", scatter_dimension=0, tiled=True
        ).astype(jnp.float32),
        lax.psum_scatter(
            over_dp[5].astype(jnp.bfloat16), "seq", scatter_dimension=0, tiled=True
        ).astype(jnp.float32),
    )
    return (
        layer_out.reshape(1, local_rows, -1),
        token_grad.reshape(1, local_rows, -1),
        attention_sums[0],
        attention_sums[1],
        attention_sums[2],
        attention_sums[3],
        gain_sums[0],
        gain_sums[1],
        attention_sums[4],
        attention_sums[5],
        feed_sums[0],
        feed_sums[1],
        feed_sums[2],
    )


def solution(mesh):
    in_specs = (
        P("dp", "seq", None),
        P("dp", None),
        P("dp", None),
        P("dp"),
        P("dp", None),
        P("dp", None),
        P("dp", None),
        P(),
        P(),
        P("dp", None),
        P("dp"),
        P("dp", None),
        P("dp", None),
        P("dp", None),
        P("dp", "seq", None),
    )
    out_specs = (
        P("dp", "seq", None),
        P("dp", "seq", None),
        P(("dp", "seq")),
        P(("dp", "seq"), None),
        P(("dp", "seq"), None),
        P(("dp", "seq"), None),
        P(),
        P(),
        P(("dp", "seq"), None),
        P(("dp", "seq")),
        P(("dp", "seq"), None),
        P(("dp", "seq"), None),
        P(("dp", "seq"), None),
    )
    return jax.shard_map(local, mesh=mesh, in_specs=in_specs, out_specs=out_specs, check_vma=False)
```

profile of v0, /device:TPU:0, one launch (start us, length us, event | category | flops | bytes accessed | tf_op | source)
XLA Modules:
  0.0 2176.2 jit_solution(12108699646013681709)
XLA Ops:
  20.1 22.3 %all-gather = bf16[8,1,128]{2,1,0:T(2,128)(2,1)S(1)} all-gather(bf16[1,1,128]{2,1,0:T(2,128)(2,1)S(1)} %convert_bitcast_fusion.4), channel_id=1, replica_groups=mesh['dp'=8,'seq'=4] {'dp'}, dimensions={0}, use_global_device_ids=true | all-gather | bytes 2304 | tf_op jit(solution)/shard_map/all_gather | solution.py:185
  43.6 10.0 all-gather.12.cloned.1.call-done
  60.8 34.4 %all-gather.14.cloned.1.call-done = bf16[1024,512]{1,0:T(8,128)(2,1)} async-done(((bf16[128,512]{1,0:T(8,128)(2,1)}), bf16[1024,512]{1,0:T(8,128)(2,1)}) %all-gather.14.cloned.1.call-update) | async-done | bytes 1048592 | tf_op jit(solution)/shard_map/all_gather | solution.py:188
  97.7 48.3 %all-gather.10.cloned.1.call-done = bf16[1024,1024]{1,0:T(8,128)(2,1)} async-done(((bf16[128,1024]{1,0:T(8,128)(2,1)}), bf16[1024,1024]{1,0:T(8,128)(2,1)}) %all-gather.10.cloned.1.call-update) | async-done | bytes 2097168 | tf_op jit(solution)/shard_map/all_gather | solution.py:186
  173.8 18.6 while.27
  207.3 18.8 all-gather.1
  229.8 104.5 %all-gather.18.cloned.1.call-done = bf16[1024,4608]{1,0:T(8,128)(2,1)} async-done(((bf16[128,4608]{1,0:T(8,128)(2,1)}), bf16[1024,4608]{1,0:T(8,128)(2,1)}) %all-gather.18.cloned.1.call-update) | async-done | bytes 9437200 | tf_op jit(solution)/shard_map/all_gather | solution.py:193
  342.2 130.4 %all-gather.20.cloned.1.call-done = bf16[1024,4608]{1,0:T(8,128)(2,1)} async-done(((bf16[128,4608]{1,0:T(8,128)(2,1)}), bf16[1024,4608]{1,0:T(8,128)(2,1)}) %all-gather.20.cloned.1.call-update) | async-done | bytes 9437200 | tf_op jit(solution)/shard_map/all_gather | solution.py:194
  480.5 130.6 %all-gather.22.cloned.1.call-done = bf16[4608,1024]{1,0:T(8,128)(2,1)} async-done(((bf16[576,1024]{1,0:T(8,128)(2,1)}), bf16[4608,1024]{1,0:T(8,128)(2,1)}) %all-gather.22.cloned.1.call-update) | async-done | bytes 9437200 | tf_op jit(solution)/shard_map/all_gather | solution.py:195
  611.1 13.4 multiply_convert_fusion
  655.2 55.5 %while.28 = (s32[]{:T(128)}, f32[1024,2,64]{0,2,1:T(8,128)S(1)}, f32[1024,2,64]{0,2,1:T(8,128)}, bf16[2,512,2,2,64]{1,4,3,2,0:T(8,128)(2,1)}, bf16[2,512,2,2,64]...) while((s32[]{:T(128)}, f32[1024,2,64]{0,2,1:T(8,128)S(1)}, ...), condition=%wide.region_13.14_spmd.clone, body=%wide.region_11.13_spmd.clone.sunk | while | flops 1377697280 | bytes 121713128 | solution.py:144
  749.3 11.2 all_to_all.110
  792.8 9.7 fusion.81
  804.3 55.4 %reduce-scatter.23.cloned.1.call-done = f32[128,512]{1,0:T(8,128)} async-done(((f32[1024,512]{1,0:T(8,128)}), f32[128,512]{1,0:T(8,128)}) %reduce-scatter.23.cloned.1.call-update) | async-done | bytes 262160 | tf_op jit(solution)/shard_map/reduce_scatter | solution.py:399
  861.5 88.9 %reduce-scatter.27.cloned.1.call-done = f32[128,1024]{1,0:T(8,128)} async-done(((f32[1024,1024]{1,0:T(8,128)}), f32[128,1024]{1,0:T(8,128)}) %reduce-scatter.27.cloned.1.call-update) | async-done | bytes 524304 | tf_op jit(solution)/shard_map/reduce_scatter | solution.py:400
  952.2 90.1 %reduce-scatter.15.cloned.1.call-done = f32[128,1024]{1,0:T(8,128)} async-done(((f32[1024,1024]{1,0:T(8,128)}), f32[128,1024]{1,0:T(8,128)}) %reduce-scatter.15.cloned.1.call-update) | async-done | bytes 524304 | tf_op jit(solution)/shard_map/reduce_scatter | solution.py:397
  1044.2 315.0 %reduce-scatter.31.cloned.1.call-done = f32[128,4608]{1,0:T(8,128)} async-done(((f32[1024,4608]{1,0:T(8,128)}), f32[128,4608]{1,0:T(8,128)}) %reduce-scatter.31.cloned.1.call-update) | async-done | bytes 2359312 | tf_op jit(solution)/shard_map/reduce_scatter | solution.py:287
  1362.0 313.4 %reduce-scatter.35.cloned.1.call-done = f32[128,4608]{1,0:T(8,128)} async-done(((f32[1024,4608]{1,0:T(8,128)}), f32[128,4608]{1,0:T(8,128)}) %reduce-scatter.35.cloned.1.call-update) | async-done | bytes 2359312 | tf_op jit(solution)/shard_map/reduce_scatter | solution.py:288
  1680.8 310.7 %reduce-scatter.39.cloned.1.call-done = f32[576,1024]{1,0:T(8,128)} async-done(((f32[4608,1024]{1,0:T(8,128)}), f32[576,1024]{1,0:T(8,128)}) %reduce-scatter.39.cloned.1.call-update) | async-done | bytes 2359312 | tf_op jit(solution)/shard_map/reduce_scatter | solution.py:289
  2004.5 19.7 all-reduce.5
  2024.3 36.8 %all-reduce.4 = (f32[64]{0:T(128)}, f32[64]{0:T(128)}) all-reduce(f32[64]{0:T(128)S(1)} %get-tuple-element.297, f32[64]{0:T(128)S(1)} %get-tuple-element.303), channel_id=1, replica_groups=mesh['dp'=8,'seq'=4] {'dp','seq'}, use_global_device_ids=true, to_apply=%region_27.28 | all-reduce | flops 128 | bytes 1024 | tf_op jit(solution)/shard_map/psum | solution.py:394
  2083.5 26.8 %reduce-scatter.33.cloned.1.call-done = bf16[32,4608]{1,0:T(8,128)(2,1)} async-done(((bf16[128,4608]{1,0:T(8,128)(2,1)}), bf16[32,4608]{1,0:T(8,128)(2,1)}) %reduce-scatter.33.cloned.1.call-update) | async-done | bytes 294928 | tf_op jit(solution)/shard_map/reduce_scatter | solution.py:292
  2112.1 26.5 %reduce-scatter.37.cloned.1.call-done = bf16[32,4608]{1,0:T(8,128)(2,1)} async-done(((bf16[128,4608]{1,0:T(8,128)(2,1)}), bf16[32,4608]{1,0:T(8,128)(2,1)}) %reduce-scatter.37.cloned.1.call-update) | async-done | bytes 294928 | tf_op jit(solution)/shard_map/reduce_scatter | solution.py:295
  2140.5 26.5 %reduce-scatter.41.cloned.1.call-done = bf16[144,1024]{1,0:T(8,128)(2,1)} async-done(((bf16[576,1024]{1,0:T(8,128)(2,1)}), bf16[144,1024]{1,0:T(8,128)(2,1)}) %reduce-scatter.41.cloned.1.call-update) | async-done | bytes 294928 | tf_op jit(solution)/shard_map/reduce_scatter | solution.py:298
  (374 shorter events, 312.3 us)
Async XLA Ops:
  7.2 46.4 %all-gather.12.cloned.1.call-start = ((), (), s32[]{:S(2)}) async-start(), calls=%async_computation.23 | async-start | bytes 1179648 | tf_op jit(solution)/shard_map/all_gather | solution.py:187
  9.0 86.2 %all-gather.14.cloned.1.call-start = ((), (), s32[]{:S(2)}) async-start(), calls=%async_computation.24 | async-start | bytes 1179648 | tf_op jit(solution)/shard_map/all_gather | solution.py:188
  10.7 135.3 %all-gather.10.cloned.1.call-start = ((), (), s32[]{:S(2)}) async-start(), calls=%async_computation.22 | async-start | bytes 2359296 | tf_op jit(solution)/shard_map/all_gather | solution.py:186
  12.6 214.4 %all-gather.16.cloned.1.call-start = ((), (), s32[]{:S(2)}) async-start(), calls=%async_computation.25 | async-start | bytes 2359296 | tf_op jit(solution)/shard_map/all_gather | solution.py:189
  14.4 319.9 %all-gather.18.cloned.1.call-start = ((), (), s32[]{:S(2)}) async-start(), calls=%async_computation.26 | async-start | bytes 10616832 | tf_op jit(solution)/shard_map/all_gather | solution.py:193
  15.7 456.9 %all-gather.20.cloned.1.call-start = ((), (), s32[]{:S(2)}) async-start(), calls=%async_computation.27 | async-start | bytes 10616832 | tf_op jit(solution)/shard_map/all_gather | solution.py:194
  18.7 592.4 %all-gather.22.cloned.1.call-start = ((), (), s32[]{:S(2)}) async-start(), calls=%async_computation.28 | async-start | bytes 10616832 | tf_op jit(solution)/shard_map/all_gather | solution.py:195
  57.4 93.6 %all-to-all-start.1 = ((bf16[256,4,128]{0,2,1:T(8,128)(2,1)}), bf16[256,4,128]{0,2,1:T(8,128)(2,1)S(1)}, u32[]{:S(2)}, u32[]{:S(2)}) async-start(bf16[256,4,128]{0,2,1:T(8,128)(2,1)} %bitcast.26), calls=%async_computation.1 | async-start | bytes 524288 | tf_op jit(solution)/shard_map/all_to_all | solution.py:221
  160.4 12.5 all-to-all-start
  203.8 22.3 %all-to-all-start.3 = ((bf16[4,2,32768]{2,1,0:T(2,128)(2,1)}), bf16[4,2,32768]{2,1,0:T(2,128)(2,1)S(1)}, u32[]{:S(2)}, u32[]{:S(2)}) async-start(bf16[4,2,32768]{2,1,0:T(2,128)(2,1)} %reshape.554), calls=%async_computation.3 | async-start | bytes 1048576 | tf_op jit(solution)/shard_map/all_to_all | solution.py:242
  641.6 161.0 %reduce-scatter.19.cloned.1.call-start = ((), (), s32[]{:S(2)}) async-start(), calls=%async_computation.31 | async-start | bytes 2359296 | tf_op jit(solution)/shard_map/reduce_scatter | solution.py:398
  724.2 135.5 %reduce-scatter.23.cloned.1.call-start = ((), (), s32[]{:S(2)}) async-start(), calls=%async_computation.33 | async-start | bytes 2359296 | tf_op jit(solution)/shard_map/reduce_scatter | solution.py:399
  736.3 214.0 %reduce-scatter.27.cloned.1.call-start = ((), (), s32[]{:S(2)}) async-start(), calls=%async_computation.35 | async-start | bytes 4718592 | tf_op jit(solution)/shard_map/reduce_scatter | solution.py:400
  739.1 303.2 %reduce-scatter.15.cloned.1.call-start = ((), (), s32[]{:S(2)}) async-start(), calls=%async_computation.29 | async-start | bytes 4718592 | tf_op jit(solution)/shard_map/reduce_scatter | solution.py:397
  772.2 586.9 %reduce-scatter.31.cloned.1.call-start = ((), (), s32[]{:S(2)}) async-start(), calls=%async_computation.37 | async-start | bytes 21233664 | tf_op jit(solution)/shard_map/reduce_scatter | solution.py:287
  781.8 893.6 %reduce-scatter.35.cloned.1.call-start = ((), (), s32[]{:S(2)}) async-start(), calls=%async_computation.39 | async-start | bytes 21233664 | tf_op jit(solution)/shard_map/reduce_scatter | solution.py:288
  791.8 1199.8 %reduce-scatter.39.cloned.1.call-start = ((), (), s32[]{:S(2)}) async-start(), calls=%async_computation.41 | async-start | bytes 21233664 | tf_op jit(solution)/shard_map/reduce_scatter | solution.py:289
  802.6 1267.0 %reduce-scatter.21.cloned.1.call-start = ((), (), s32[]{:S(2)}) async-start(), calls=%async_computation.32 | async-start | bytes 163840 | tf_op jit(solution)/shard_map/reduce_scatter | solution.py:410
  804.3 1266.7 %reduce-scatter.25.cloned.1.call-start = ((), (), s32[]{:S(2)}) async-start(), calls=%async_computation.34 | async-start | bytes 163840 | tf_op jit(solution)/shard_map/reduce_scatter | solution.py:413
  861.4 1211.0 %reduce-scatter.29.cloned.1.call-start = ((), (), s32[]{:S(2)}) async-start(), calls=%async_computation.36 | async-start | bytes 327680 | tf_op jit(solution)/shard_map/reduce_scatter | solution.py:416
  952.1 1129.8 %reduce-scatter.17.cloned.1.call-start = ((), (), s32[]{:S(2)}) async-start(), calls=%async_computation.30 | async-start | bytes 327680 | tf_op jit(solution)/shard_map/reduce_scatter | solution.py:407
  1044.1 1066.2 %reduce-scatter.33.cloned.1.call-start = ((), (), s32[]{:S(2)}) async-start(), calls=%async_computation.38 | async-start | bytes 1474560 | tf_op jit(solution)/shard_map/reduce_scatter | solution.py:292
  1361.9 776.7 %reduce-scatter.37.cloned.1.call-start = ((), (), s32[]{:S(2)}) async-start(), calls=%async_computation.40 | async-start | bytes 1474560 | tf_op jit(solution)/shard_map/reduce_scatter | solution.py:295
  1678.3 488.8 %reduce-scatter.41.cloned.1.call-start = ((), (), s32[]{:S(2)}) async-start(), calls=%async_computation.42 | async-start | bytes 1474560 | tf_op jit(solution)/shard_map/reduce_scatter | solution.py:298
  (69 other events, 3847.9 us)
Sparse Core Ops, SparseCore 0:
  10.7 42.8 all-gather.11
  56.3 38.8 all-gather.13
  97.9 48.0 all-gather.9
  148.0 47.7 all-gather.15
  197.8 136.4 all-gather.17
  336.3 136.2 all-gather.19
  474.8 136.2 all-gather.21
  724.4 65.0 reduce-scatter.18
  793.0 66.6 reduce-scatter.22
  863.2 87.0 reduce-scatter.26
  954.4 87.8 reduce-scatter.14
  1046.0 313.0 reduce-scatter.30
  1363.0 312.4 reduce-scatter.34
  1679.2 312.3 reduce-scatter.38
  1994.4 18.7 reduce-scatter.20
  2016.1 19.6 reduce-scatter.24
  2038.7 20.0 reduce-scatter.28
  2061.8 20.1 reduce-scatter.16
  2084.5 25.7 reduce-scatter.32
  2112.9 25.7 reduce-scatter.36
  2141.3 25.7 reduce-scatter.40
where the time goes:
time: 2180 us
  waiting for transfers between devices  1740 us (80%)
  matrix products  145 us (7%)
  blocking collectives  133 us (6%)
  other arithmetic  72.8 us (3%)
  local copies, waits for them, and re-layouts  44.7 us (2%)
    reduce_scatter x1, waiting for transfers between devices, local(): lax.psum_scatter(gate_grad, 'dp', scatter_dimension=0, tiled=True)  315 us
    reduce_scatter x1, waiting for transfers between devices, local(): lax.psum_scatter(up_grad, 'dp', scatter_dimension=0, tiled=True)  313 us
    reduce_scatter x1, waiting for transfers between devices, local(): lax.psum_scatter(down_grad, 'dp', scatter_dimension=0, tiled=True)  311 us
    all_gather x1, waiting for transfers between devices, local(): lax.all_gather(down_weight.astype(jnp.bfloat16), 'dp', axis=0, tiled=True)  131 us
    all_gather x1, waiting for transfers between devices, local(): lax.all_gather(up_weight.astype(jnp.bfloat16), 'dp', axis=0, tiled=True)  130 us
    all_gather x1, waiting for transfers between devices, local(): lax.all_gather(gate_weight.astype(jnp.bfloat16), 'dp', axis=0, tiled=True)  105 us
    reduce_scatter x1, waiting for transfers between devices, local(): lax.psum_scatter(query_w_grad, 'dp', scatter_dimension=0, tiled=True)  90.1 us
    reduce_scatter x1, waiting for transfers between devices, local(): lax.psum_scatter(output_grad, 'dp', scatter_dimension=0, tiled=True)  88.9 us
  transfers between devices with their start and end apart: 26, of which 19 were waited for; matrix products, arithmetic and copies ran while one was open for 8% of the time, Pallas kernels for 0%

commit v1 on v0

v1 whole, which is shorter than its diff:
```python
import math

import jax
import jax.numpy as jnp
from jax import lax
from jax.sharding import PartitionSpec as P

EPS = 1e-05
ROPE_BASE = 1000000.0
NEG_FILL = -1e30
BF = jnp.bfloat16
F32 = jnp.float32


def dot(left, right, dims):
    return lax.dot_general(left, right, (dims, ((), ())), preferred_element_type=F32)


def mm(left, right):
    return dot(left, right, ((1,), (0,)))


def mm_nt(left, right):
    return dot(left, right, ((1,), (1,)))


def mm_tn(left, right):
    return dot(left, right, ((0,), (0,)))


def rms_stats(values):
    factor = lax.rsqrt(jnp.mean(values * values, axis=-1, keepdims=True) + EPS)
    return (values * factor, factor)


def rms_back(grad_unit, unit_values, factor):
    return factor * (
        grad_unit - unit_values * jnp.mean(grad_unit * unit_values, axis=-1, keepdims=True)
    )


def doc_positions(segment_row):
    length = segment_row.shape[0]
    places = jnp.arange(length, dtype=jnp.int32)
    change = jnp.concatenate([jnp.ones((1,), dtype=jnp.bool_), segment_row[1:] != segment_row[:-1]])
    starts = lax.cummax(jnp.where(change, places, jnp.zeros_like(places)), axis=0)
    return places - starts


def rope_tables(positions, half_dim):
    frequency = ROPE_BASE ** (-jnp.arange(half_dim, dtype=F32) / half_dim)
    angles = positions.astype(F32)[:, None] * frequency[None, :]
    return (jnp.cos(angles), jnp.sin(angles))


def rotate(values, cos_table, sin_table):
    half_dim = values.shape[-1] // 2
    first_half = values[..., :half_dim]
    second_half = values[..., half_dim:]
    cos_wide = cos_table[:, None, :]
    sin_wide = sin_table[:, None, :]
    return jnp.concatenate(
        [
            first_half * cos_wide - second_half * sin_wide,
            second_half * cos_wide + first_half * sin_wide,
        ],
        axis=-1,
    )


def block_mask(segment_row, valid_row, first_row, block_rows):
    length = segment_row.shape[0]
    columns = jnp.arange(length, dtype=jnp.int32)
    rows_here = first_row + jnp.arange(block_rows, dtype=jnp.int32)
    segment_here = lax.dynamic_slice_in_dim(segment_row, first_row, block_rows, 0)
    return (columns[None, :] <= rows_here[:, None]) & (
        segment_here[:, None] == segment_row[None, :]
    ) & (valid_row[None, :] > 0) | (columns[None, :] == rows_here[:, None])


def block_scores(query_block, keys_all, allowed, score_scale):
    scores = (
        jnp.einsum("qgrd,kgd->grqk", query_block, keys_all, preferred_element_type=F32)
        * score_scale
    )
    return jnp.where(allowed[None, None], scores, NEG_FILL)


def attention_forward(queries, keys_all, values_all, segment_row, valid_row, score_scale):
    block_count = queries.shape[0]
    block_rows = queries.shape[1]

    def one_block(block_items):
        query_block, block_index = block_items
        allowed = block_mask(segment_row, valid_row, block_index * block_rows, block_rows)
        scores = block_scores(query_block, keys_all, allowed, score_scale)
        largest = jnp.max(scores, axis=-1, keepdims=True)
        weights_exp = jnp.exp(scores - largest)
        totals = jnp.sum(weights_exp, axis=-1, keepdims=True)
        shares = (weights_exp / totals).astype(BF)
        mixed_block = jnp.einsum("grqk,kgd->qgrd", shares, values_all, preferred_element_type=F32)
        return (mixed_block.astype(BF), (largest + jnp.log(totals))[..., 0])

    return lax.map(one_block, (queries, jnp.arange(block_count, dtype=jnp.int32)))


def attention_backward(
    queries, keys_all, values_all, grad_out, log_totals, segment_row, valid_row, score_scale
):
    block_count = queries.shape[0]
    block_rows = queries.shape[1]

    def one_block(running, block_items):
        key_sum, value_sum = running
        query_block, grad_block, log_block, block_index = block_items
        allowed = block_mask(segment_row, valid_row, block_index * block_rows, block_rows)
        scores = block_scores(query_block, keys_all, allowed, score_scale)
        shares = jnp.exp(scores - log_block[..., None])
        grad_shares = jnp.einsum(
            "qgrd,kgd->grqk", grad_block, values_all, preferred_element_type=F32
        )
        centre = jnp.sum(shares * grad_shares, axis=-1, keepdims=True)
        grad_scores = (shares * (grad_shares - centre)).astype(BF)
        grad_query = (
            jnp.einsum("grqk,kgd->qgrd", grad_scores, keys_all, preferred_element_type=F32)
            * score_scale
        )
        key_sum = (
            key_sum
            + jnp.einsum("grqk,qgrd->kgd", grad_scores, query_block, preferred_element_type=F32)
            * score_scale
        )
        value_sum = value_sum + jnp.einsum(
            "grqk,qgrd->kgd", shares.astype(BF), grad_block, preferred_element_type=F32
        )
        return ((key_sum, value_sum), grad_query.astype(BF))

    zero_keys = jnp.zeros(keys_all.shape, F32)
    zero_values = jnp.zeros(values_all.shape, F32)
    sums_out, query_grad = lax.scan(
        one_block,
        (zero_keys, zero_values),
        (queries, grad_out, log_totals, jnp.arange(block_count, dtype=jnp.int32)),
    )
    return (sums_out[0], sums_out[1], query_grad)


def swap(values, bit):
    count = lax.axis_size("seq")
    return lax.ppermute(values, "seq", [(i, i ^ bit) for i in range(count)])


def seq_gather(values):
    count = lax.axis_size("seq")
    if count != 4:
        return lax.all_gather(values, "seq", axis=0)
    place = lax.axis_index("seq")
    far = swap(values, 2)
    near = swap(values, 1)
    far_near = swap(far, 1)
    odd = (place & 1) == 1
    high = place >= 2
    mine = (jnp.where(odd, near, values), jnp.where(odd, values, near))
    theirs = (jnp.where(odd, far_near, far), jnp.where(odd, far, far_near))
    return jnp.stack(
        [
            jnp.where(high, theirs[0], mine[0]),
            jnp.where(high, theirs[1], mine[1]),
            jnp.where(high, mine[0], theirs[0]),
            jnp.where(high, mine[1], theirs[1]),
        ]
    )


def seq_scatter(values):
    count = lax.axis_size("seq")
    if count != 4:
        return lax.psum_scatter(
            values.astype(BF), "seq", scatter_dimension=0, tiled=True
        ).astype(F32)
    place = lax.axis_index("seq")
    rows = values.shape[0] // 4
    split = values.reshape(2, 2, rows, -1)
    odd = (place & 1) == 1
    high = place >= 2
    keep = jnp.where(odd, split[:, 1], split[:, 0])
    send = jnp.where(odd, split[:, 0], split[:, 1]).astype(BF)
    pair = keep + swap(send, 1).astype(F32)
    keep = jnp.where(high, pair[1], pair[0])
    send = jnp.where(high, pair[0], pair[1]).astype(BF)
    return keep + swap(send, 2).astype(F32)


def dp_gather(values):
    return lax.all_gather(values, "dp", axis=0, tiled=True)


def dp_scatter(values):
    return lax.psum_scatter(values.astype(BF), "dp", scatter_dimension=0, tiled=True)


def sum_all(values):
    for axis in ("seq", "dp"):
        count = lax.axis_size(axis)
        bit = 1
        while bit < count:
            values = values + lax.ppermute(values, axis, [(i, i ^ bit) for i in range(count)])
            bit *= 2
    return values


def local(
    tokens,
    segments,
    valid_mask,
    attention_gain,
    query_weight,
    key_weight,
    value_weight,
    query_gain,
    key_gain,
    output_weight,
    feedforward_gain,
    gate_weight,
    up_weight,
    down_weight,
    cotangent,
):
    seq_count = lax.axis_size("seq")
    dp_count = lax.axis_size("dp")
    place = lax.axis_index("seq")
    local_rows = tokens.shape[1]
    row_length = segments.shape[1]
    head_dim = query_gain.shape[0]
    width = tokens.shape[2]
    hidden_width = gate_weight.shape[1]
    query_width = query_weight.shape[1]
    key_width = key_weight.shape[1]
    query_here = query_width // seq_count
    key_here = key_width // seq_count
    hidden_here = hidden_width // seq_count
    heads_here = query_here // head_dim
    groups_here = key_here // head_dim
    group_size = heads_here // groups_here
    weight_rows = query_weight.shape[0]
    own_rows = weight_rows // seq_count
    block_rows = min(512, row_length)
    block_count = row_length // block_rows
    score_scale = 1.0 / math.sqrt(head_dim)
    segment_row = segments[0]
    valid_row = valid_mask[0]

    def columns_of(weight, size):
        return lax.dynamic_slice_in_dim(weight, place * size, size, 1)

    def low(weight):
        return weight.astype(BF).astype(F32)

    gain_one = low(attention_gain)[:, None]
    gain_two = low(feedforward_gain)[:, None]
    attention_pack = jnp.concatenate(
        [
            (low(columns_of(query_weight, query_here)) * gain_one).astype(BF),
            (low(columns_of(key_weight, key_here)) * gain_one).astype(BF),
            (low(columns_of(value_weight, key_here)) * gain_one).astype(BF),
            columns_of(output_weight, width // seq_count).astype(BF),
        ],
        axis=1,
    )
    piece = hidden_width // (dp_count * seq_count)

    def hidden_columns(weight):
        split = weight.reshape(weight_rows, dp_count, seq_count, piece)
        mine = lax.dynamic_index_in_dim(split, place, 2, keepdims=False)
        return (low(mine.reshape(weight_rows, hidden_here)) * gain_two).astype(BF)

    gate_up_pack = jnp.concatenate([hidden_columns(gate_weight), hidden_columns(up_weight)], axis=1)
    down_pack = lax.dynamic_slice_in_dim(down_weight, place * piece, piece, 0).astype(BF)

    attention_all = dp_gather(attention_pack)
    gate_up_all = dp_gather(gate_up_pack)
    down_all = dp_gather(down_pack)

    inputs = seq_gather(tokens[0]).reshape(row_length, width).astype(F32)
    qkv_width = query_here + 2 * key_here
    qkv_weight = attention_all[:, :qkv_width]
    output_all = jnp.concatenate(list(seq_gather(attention_all[:, qkv_width:])), axis=1)
    grad_rows = seq_gather(cotangent[0]).reshape(row_length, width)

    positions = doc_positions(segment_row)
    cos_table, sin_table = rope_tables(positions, head_dim // 2)
    unit_one = rms_stats(inputs)[0].astype(BF)
    qkv_raw = mm(unit_one, qkv_weight)
    query_raw = qkv_raw[:, :query_here].reshape(row_length, heads_here, head_dim)
    key_raw = qkv_raw[:, query_here : query_here + key_here].reshape(
        row_length, groups_here, head_dim
    )
    values_all = (
        qkv_raw[:, query_here + key_here :].astype(BF).reshape(row_length, groups_here, head_dim)
    )
    query_unit, query_factor = rms_stats(query_raw)
    key_unit, key_factor = rms_stats(key_raw)
    queries = rotate(query_unit * query_gain, cos_table, sin_table).astype(BF)
    keys_all = rotate(key_unit * key_gain, cos_table, sin_table).astype(BF)
    query_blocks = queries.reshape(block_count, block_rows, groups_here, group_size, head_dim)
    mixed_blocks, log_totals = attention_forward(
        query_blocks, keys_all, values_all, segment_row, valid_row, score_scale
    )
    mixed_here = mixed_blocks.reshape(row_length, query_here)
    mixed_all = jnp.concatenate(list(seq_gather(mixed_here)), axis=1)
    after_attention = inputs + mm(mixed_all, output_all)
    unit_two = rms_stats(after_attention)[0].astype(BF)

    gate_up = mm(unit_two, gate_up_all)
    gate_value = gate_up[:, :hidden_here]
    up_value = gate_up[:, hidden_here:]
    sigmoid_gate = jax.nn.sigmoid(gate_value)
    silu_gate = gate_value * sigmoid_gate
    hidden = (silu_gate * up_value).astype(BF)
    grad_hidden = mm_nt(grad_rows, down_all)
    grad_gate = (
        grad_hidden * up_value * sigmoid_gate * (1.0 + gate_value * (1.0 - sigmoid_gate))
    ).astype(BF)
    grad_up = (grad_hidden * silu_gate).astype(BF)
    grad_gate_up = jnp.concatenate([grad_gate, grad_up], axis=1)
    grad_normed = seq_scatter(mm_nt(grad_gate_up, gate_up_all))

    down_sums = dp_scatter(mm_tn(hidden, grad_rows))
    gate_up_sums = dp_scatter(mm_tn(unit_two, grad_gate_up))

    after_here = lax.dynamic_slice_in_dim(after_attention, place * local_rows, local_rows, 0)
    layer_out = (after_here + seq_scatter(mm(hidden, down_all))).astype(BF)

    unit_here, factor_here = rms_stats(after_here)
    grad_after = cotangent[0].astype(F32) + rms_back(grad_normed, unit_here, factor_here)
    grad_branch = seq_gather(grad_after.astype(BF)).reshape(row_length, width)
    output_here = lax.dynamic_slice_in_dim(output_all, place * query_here, query_here, 0)
    grad_mixed = mm_nt(grad_branch, output_here).astype(BF)
    output_sums = dp_scatter(mm_tn(mixed_here, grad_branch))

    grad_blocks = grad_mixed.reshape(block_count, block_rows, groups_here, group_size, head_dim)
    key_sum, value_sum, query_grad = attention_backward(
        query_blocks,
        keys_all,
        values_all,
        grad_blocks,
        log_totals,
        segment_row,
        valid_row,
        score_scale,
    )
    query_turned = rotate(
        query_grad.reshape(row_length, heads_here, head_dim).astype(F32), cos_table, -sin_table
    )
    key_turned = rotate(key_sum.astype(BF).astype(F32), cos_table, -sin_table)
    gain_terms = jnp.stack(
        [
            jnp.sum(query_turned * query_unit, axis=(0, 1)),
            jnp.sum(key_turned * key_unit, axis=(0, 1)),
        ]
    )
    qkv_grad = jnp.concatenate(
        [
            rms_back(query_turned * query_gain, query_unit, query_factor)
            .astype(BF)
            .reshape(row_length, query_here),
            rms_back(key_turned * key_gain, key_unit, key_factor)
            .astype(BF)
            .reshape(row_length, key_here),
            value_sum.astype(BF).reshape(row_length, key_here),
        ],
        axis=1,
    )
    qkv_sums = dp_scatter(mm_tn(unit_one, qkv_grad))
    grad_one = seq_scatter(mm_nt(qkv_grad, qkv_weight))
    unit_tokens, factor_tokens = rms_stats(tokens[0].astype(F32))
    token_grad = (grad_after + rms_back(grad_one, unit_tokens, factor_tokens)).astype(BF)
    gain_sums = sum_all(gain_terms)

    def to_owners(sums):
        return lax.all_to_all(
            sums.reshape(seq_count, own_rows, -1), "seq", split_axis=0, concat_axis=0, tiled=True
        ).astype(F32)

    def own(weight):
        return lax.dynamic_slice_in_dim(weight, place * own_rows, own_rows, 0)

    def joined(pieces):
        return jnp.swapaxes(pieces, 0, 1).reshape(own_rows, -1)

    qkv_own = to_owners(qkv_sums)
    query_own = joined(qkv_own[:, :, :query_here])
    key_own = joined(qkv_own[:, :, query_here : query_here + key_here])
    value_own = joined(qkv_own[:, :, query_here + key_here :])
    gain_one_own = own(gain_one)
    attention_gain_grad = (
        jnp.sum(own(low(query_weight)) * query_own, axis=1)
        + jnp.sum(own(low(key_weight)) * key_own, axis=1)
        + jnp.sum(own(low(value_weight)) * value_own, axis=1)
    )

    hidden_own = to_owners(gate_up_sums).reshape(seq_count, own_rows, 2, dp_count, piece)
    hidden_own = jnp.transpose(hidden_own, (2, 1, 3, 0, 4)).reshape(2, own_rows, hidden_width)
    gain_two_own = own(gain_two)
    feed_gain_grad = jnp.sum(own(low(gate_weight)) * hidden_own[0], axis=1) + jnp.sum(
        own(low(up_weight)) * hidden_own[1], axis=1
    )

    moves = [
        (dp * seq_count + seq, seq * dp_count + dp)
        for dp in range(dp_count)
        for seq in range(seq_count)
    ]
    output_own = lax.ppermute(output_sums, ("dp", "seq"), moves).astype(F32)

    return (
        layer_out.reshape(1, local_rows, -1),
        token_grad.reshape(1, local_rows, -1),
        attention_gain_grad,
        query_own * gain_one_own,
        key_own * gain_one_own,
        value_own * gain_one_own,
        gain_sums[0],
        gain_sums[1],
        output_own,
        feed_gain_grad,
        hidden_own[0] * gain_two_own,
        hidden_own[1] * gain_two_own,
        down_sums.astype(F32),
    )


def solution(mesh):
    in_specs = (
        P("dp", "seq", None),
        P("dp", None),
        P("dp", None),
        P("dp"),
        P("dp", None),
        P("dp", None),
        P("dp", None),
        P(),
        P(),
        P("dp", None),
        P("dp"),
        P("dp", None),
        P("dp", None),
        P("dp", None),
        P("dp", "seq", None),
    )
    out_specs = (
        P("dp", "seq", None),
        P("dp", "seq", None),
        P(("dp", "seq")),
        P(("dp", "seq"), None),
        P(("dp", "seq"), None),
        P(("dp", "seq"), None),
        P(),
        P(),
        P(("dp", "seq"), None),
        P(("dp", "seq")),
        P(("dp", "seq"), None),
        P(("dp", "seq"), None),
        P(("dp", "seq"), None),
    )
    return jax.shard_map(local, mesh=mesh, in_specs=in_specs, out_specs=out_specs, check_vma=False)
```

time: 2180 us -> 603 us (0.28)
  waiting for transfers between devices: 1740 us -> 345 us
  blocking collectives: 133 us -> 0 us
  matrix products: 145 us -> 100 us
    reduce_scatter x14 -> x4, waiting for transfers between devices: 1260 us -> 176 us  [dp_scatter(): lax.psum_scatter(values.astype(BF), 'dp', scatter_dimension=0, tiled=True)]
    all_gather x7 -> x3, waiting for transfers between devices: 458 us -> 71.7 us  [dp_gather(): return lax.all_gather(values, 'dp', axis=0, tiled=True)]
    ppermute x0 -> x27, waiting for transfers between devices: none -> 90.3 us  [the longest x21 79.8 us: swap(): return lax.ppermute(values, 'seq', [(i, i ^ bit) for i in range(count)])]
    all_gather x2 -> x0, blocking collectives: 41 us -> none  [the longest x1 22.3 us: local(): lax.all_gather(attention_gain.astype(jnp.bfloat16), 'dp', axis=0, tiled=T...]
    psum x1 -> x0, blocking collectives: 36.8 us -> none  [local(): gain_sums = lax.psum((query_gain_term, key_gain_term), ('dp', 'seq'))]
    dot_general x25 -> x16, matrix products: 110 us -> 73.4 us  [the longest x12 60.2 us: dot(): lax.dot_general(left, right, (dims, ((), ())), preferred_element_type=F32)]
    convert_element_type x34 -> x21, other arithmetic: 48.7 us -> 17.5 us  [the longest x2 7.39 us: one_block(): grad_scores = (shares * (grad_shares - centre)).astype(BF)]
    all_to_all x3 -> x0, blocking collectives: 28.3 us -> none  [the longest x1 11.2 us: local(): lax.all_to_all(query_grad.reshape(row_length, 1, -1), 'seq', split_axis=0...]
  transfers between devices with their start and end apart: 26 -> 36, of which waited for: 19 -> 22; matrix products, arithmetic and copies ran while one was open for 8% -> 26% of each run, Pallas kernels for 0% -> 0%
where the time goes in v1:
time: 603 us; the launch traced here: 596 us
  waiting for transfers between devices  345 us (57%)
  matrix products  100 us (17%)
  other arithmetic  59.3 us (10%)
  local copies, waits for them, and re-layouts  46 us (8%)
  starting transfers between devices  26.6 us (4%)
  between operations  15.6 us (3%)
    reduce_scatter x4, waiting for transfers between devices, dp_scatter(): lax.psum_scatter(values.astype(BF), 'dp', scatter_dimension=0, tiled=True)  176 us
    ppermute x21, waiting for transfers between devices, swap(): return lax.ppermute(values, 'seq', [(i, i ^ bit) for i in range(count)])  79.8 us
    all_gather x3, waiting for transfers between devices, dp_gather(): return lax.all_gather(values, 'dp', axis=0, tiled=True)  71.7 us
    dot_general x12, matrix products, dot(): lax.dot_general(left, right, (dims, ((), ())), preferred_element_type=F32)  60.2 us
    unnamed x105, local copies, waits for them, and re-layouts  19.5 us
    ppermute x21, starting transfers between devices, swap(): return lax.ppermute(values, 'seq', [(i, i ^ bit) for i in range(count)])  13 us
  transfers between devices with their start and end apart: 36, of which 22 were waited for; matrix products, arithmetic and copies ran while one was open for 26% of the time, Pallas kernels for 0%

profile of v1, /device:TPU:0, one launch (start us, length us, event | category | flops | bytes accessed | tf_op | source)
XLA Modules:
  0.0 596.0 jit_solution(13394205707990954879)
XLA Ops:
  24.1 10.7 %collective-permute-done = bf16[256,1024]{1,0:T(8,128)(2,1)} collective-permute-done((bf16[256,1024]{1,0:T(8,128)(2,1)S(1)}, bf16[256,1024]{1,0:T(8,128)(2,1)}, u32[]{:S(2)}, u32[]{:S(2)}) %collective-permute-start) | collective-permute-done | bytes 524320 | tf_op jit(solution)/shard_map/ppermute | solution.py:150
  34.9 10.4 %collective-permute-done.11 = bf16[256,1024]{1,0:T(8,128)(2,1)} collective-permute-done((bf16[256,1024]{1,0:T(8,128)(2,1)S(1)}, bf16[256,1024]{1,0:T(8,128)(2,1)}, u32[]{:S(2)}, u32[]{:S(2)}) %collective-permute-start.11) | collective-permute-done | bytes 524320 | tf_op jit(solution)/shard_map/ppermute | solution.py:150
  53.3 6.0 %all-gather.4.cloned.1.call-done = bf16[1024,768]{0,1:T(8,128)(2,1)} async-done(((bf16[128,768]{0,1:T(8,128)(2,1)}), bf16[1024,768]{0,1:T(8,128)(2,1)}) %all-gather.4.cloned.1.call-update) | async-done | bytes 1572880 | tf_op jit(solution)/shard_map/all_gather | solution.py:195
  65.3 18.7 %while.27 = (s32[]{:T(128)}, bf16[2,512,2,2,64]{1,4,3,2,0:T(8,128)(2,1)S(1)}, f32[2,2,2,512]{3,2,1,0:T(2,128)S(1)}, s32[2]{0:T(128)S(1)}, s32[1024]{0:T(1024)S(1...) while((s32[]{:T(128)}, ...), condition=%wide.region_8.9_spmd, body=%wide.region_5.8_spmd.sunk | while | flops 565313024 | bytes 28397780 | solution.py:104
  87.9 11.7 %collective-permute-done.3 = bf16[1024,256]{0,1:T(8,128)(2,1)S(1)} collective-permute-done((bf16[1024,256]{0,1:T(8,128)(2,1)S(1)}, bf16[1024,256]{0,1:T(8,128)(2,1)S(1)}, u32[]{:S(2)}, u32[]{:S(2)}) %collective-permute-start.3) | collective-permute-done | bytes 524320 | tf_op jit(solution)/shard_map/ppermute | solution.py:150
  100.1 8.7 %collective-permute-done.6 = bf16[1024,256]{0,1:T(8,128)(2,1)S(1)} collective-permute-done((bf16[1024,256]{0,1:T(8,128)(2,1)S(1)}, bf16[1024,256]{0,1:T(8,128)(2,1)S(1)}, u32[]{:S(2)}, u32[]{:S(2)}) %collective-permute-start.6) | collective-permute-done | bytes 524320 | tf_op jit(solution)/shard_map/ppermute | solution.py:150
  112.4 4.5 multiply_reduce_fusion
  116.9 24.3 %all-gather.6.cloned.1.call-done = bf16[1024,2304]{0,1:T(8,128)(2,1)} async-done(((bf16[128,2304]{0,1:T(8,128)(2,1)}), bf16[1024,2304]{0,1:T(8,128)(2,1)}) %all-gather.6.cloned.1.call-update) | async-done | bytes 4718608 | tf_op jit(solution)/shard_map/all_gather | solution.py:195
  141.2 11.0 %fusion.115 = f32[1024,2304]{1,0:T(8,128)} fusion(bf16[1024,2304]{0,1:T(8,128)(2,1)} %all-gather.6.cloned.1.call-done, f32[1024,1024]{1,0:T(8,128)} %get-tuple-element.363, f32[1024]{0:T(1024)S(1)} %add_rsqrt_fusion.2), kind=kOutput, calls=%fused_computation.297 | convolution fusion | flops 4833935360 | bytes 18354176 | tf_op jit(solution)/shard_map/dot_general | solution.py:16
  152.2 41.4 %all-gather.8.cloned.1.call-done = bf16[1152,1024]{1,0:T(8,128)(2,1)} async-done(((bf16[144,1024]{1,0:T(8,128)(2,1)}), bf16[1152,1024]{1,0:T(8,128)(2,1)}) %all-gather.8.cloned.1.call-update) | async-done | bytes 2359312 | tf_op jit(solution)/shard_map/all_gather | solution.py:195
  193.7 9.4 %multiply_convert_fusion.1 = (bf16[1024,1152]{1,0:T(8,128)(2,1)S(1)}, bf16[1024,1152]{1,0:T(8,128)(2,1)S(1)}, bf16[1024,1152]{1,0:T(8,128)(2,1)S(1)}) fusion(f32[1024,2304]{1,0:T(8,128)} %fusion.115, bf16[1024,1024]{1,0:T(8,128)(2,1)} %bitcast.470, bf16[1152,1024]{1,0:T(8,128)(2,1)} %all-gather.8.cloned.1.call-done), kind=kOutput, calls=%fused_computation.76 | convolution fusion | flops 2433613824 | bytes 20971520 | tf_op jit(solution)/shard_map/dot_general | solution.py:16
  203.2 5.0 fusion.62
  218.1 10.8 %collective-permute-done.15 = bf16[256,1024]{1,0:T(8,128)(2,1)S(1)} collective-permute-done((bf16[256,1024]{1,0:T(8,128)(2,1)S(1)}, bf16[256,1024]{1,0:T(8,128)(2,1)S(1)}, u32[]{:S(2)}, u32[]{:S(2)}) %collective-permute-start.15) | collective-permute-done | bytes 524320 | tf_op jit(solution)/shard_map/ppermute | solution.py:150
  229.2 10.5 %collective-permute-done.10 = bf16[256,1024]{1,0:T(8,128)(2,1)S(1)} collective-permute-done((bf16[256,1024]{1,0:T(8,128)(2,1)S(1)}, bf16[256,1024]{1,0:T(8,128)(2,1)S(1)}, u32[]{:S(2)}, u32[]{:S(2)}) %collective-permute-start.10) | collective-permute-done | bytes 524320 | tf_op jit(solution)/shard_map/ppermute | solution.py:150
  243.0 12.4 %collective-permute-done.16 = bf16[256,1024]{1,0:T(8,128)(2,1)} collective-permute-done((bf16[256,1024]{1,0:T(8,128)(2,1)}, bf16[256,1024]{1,0:T(8,128)(2,1)}, u32[]{:S(2)}, u32[]{:S(2)}) %collective-permute-start.16) | collective-permute-done | bytes 524320 | tf_op jit(solution)/shard_map/ppermute | solution.py:150
  269.6 43.0 %while.28 = (s32[]{:T(128)}, f32[1024,2,64]{0,2,1:T(8,128)S(1)}, f32[1024,2,64]{0,2,1:T(8,128)}, bf16[2,512,2,2,64]{1,4,3,2,0:T(8,128)(2,1)S(1)}, bf16[2,512,2,2...) while((s32[]{:T(128)}, f32[1024,2,64]{0,2,1:T(8,128)S(1)}, ...), condition=%wide.region_15.16_spmd.clone, body=%wide.region_13.15_spmd.clone.sunk | while | flops 1377697280 | bytes 136393008 | solution.py:140
  283.3 4.0 fusion.172
  308.2 4.2 fusion.171
  323.4 5.7 convolution_convert_fusion.1
  329.8 11.0 %convolution_convert_fusion = bf16[1024,2304]{1,0:T(8,128)(2,1)} fusion(bf16[1024,1152]{1,0:T(8,128)(2,1)} %copy-done.47, bf16[1024,1152]{1,0:T(8,128)(2,1)} %copy-done.46, f32[1024,1024]{1,0:T(8,128)} %get-tuple-element.363, f32[1024]{0:T(1024)S(1)} %copy-done.37), kind=kOutput, calls=%fused_computation.73 | convolution fusion | flops 4845731840 | bytes 13635584 | tf_op jit(solution)/shard_map/dot_general | solution.py:16
  374.6 15.5 %reduce-scatter.5.cloned.1.call-done = bf16[128,512]{1,0:T(8,128)(2,1)} async-done(((bf16[1024,512]{1,0:T(8,128)(2,1)}), bf16[128,512]{1,0:T(8,128)(2,1)}) %reduce-scatter.5.cloned.1.call-update) | async-done | bytes 131088 | tf_op jit(solution)/shard_map/reduce_scatter | solution.py:199
  395.8 65.9 %reduce-scatter.11.cloned.1.call-done = bf16[144,1024]{1,0:T(8,128)(2,1)} async-done(((bf16[1152,1024]{1,0:T(8,128)(2,1)}), bf16[144,1024]{1,0:T(8,128)(2,1)}) %reduce-scatter.11.cloned.1.call-update) | async-done | bytes 294928 | tf_op jit(solution)/shard_map/reduce_scatter | solution.py:199
  465.3 94.3 %reduce-scatter.9.cloned.1.call-done = bf16[128,2304]{1,0:T(8,128)(2,1)} async-done(((bf16[1024,2304]{1,0:T(8,128)(2,1)}), bf16[128,2304]{1,0:T(8,128)(2,1)}) %reduce-scatter.9.cloned.1.call-update) | async-done | bytes 589840 | tf_op jit(solution)/shard_map/reduce_scatter | solution.py:199
  565.6 7.3 %all-to-all-done.1 = bf16[4,32,2304]{2,1,0:T(8,128)(2,1)S(1)} async-done(((bf16[4,32,2304]{2,1,0:T(8,128)(2,1)}), bf16[4,32,2304]{2,1,0:T(8,128)(2,1)S(1)}, u32[]{:S(2)}, u32[]{:S(2)}) %all-to-all-start.1) | async-done | bytes 589856 | tf_op jit(solution)/shard_map/all_to_all | solution.py:381
  (341 shorter events, 192.5 us)
Async XLA Ops:
  7.2 52.2 %all-gather.4.cloned.1.call-start = ((), (), s32[]{:S(2)}) async-start(), calls=%async_computation.6 | async-start | bytes 1769472 | tf_op jit(solution)/shard_map/all_gather | solution.py:195
  11.2 130.0 %all-gather.6.cloned.1.call-start = ((), (), s32[]{:S(2)}) async-start(), calls=%async_computation.7 | async-start | bytes 5308416 | tf_op jit(solution)/shard_map/all_gather | solution.py:195
  18.9 174.7 %all-gather.8.cloned.1.call-start = ((), (), s32[]{:S(2)}) async-start(), calls=%async_computation.8 | async-start | bytes 2654208 | tf_op jit(solution)/shard_map/all_gather | solution.py:195
  19.0 15.9 %collective-permute-start = (bf16[256,1024]{1,0:T(8,128)(2,1)S(1)}, bf16[256,1024]{1,0:T(8,128)(2,1)}, u32[]{:S(2)}, u32[]{:S(2)}) collective-permute-start(bf16[256,1024]{1,0:T(8,128)(2,1)S(1)} %bitcast.463), channel_id=1, source_target_pairs={{0,2},{1,3},{2,0},{3,1},{4,6},{5,7},{6,4},{7,5},{8,10},{9,11},{10,... | collective-permute-start | bytes 1572872 | tf_op jit(solution)/shard_map/ppermute | solution.py:150
  22.0 23.3 %collective-permute-start.11 = (bf16[256,1024]{1,0:T(8,128)(2,1)S(1)}, bf16[256,1024]{1,0:T(8,128)(2,1)}, u32[]{:S(2)}, u32[]{:S(2)}) collective-permute-start(bf16[256,1024]{1,0:T(8,128)(2,1)S(1)} %bitcast.475), channel_id=1, source_target_pairs={{0,2},{1,3},{2,0},{3,1},{4,6},{5,7},{6,4},{7,5},{8,10},{9,11},{10,... | collective-permute-start | bytes 1572872 | tf_op jit(solution)/shard_map/ppermute | solution.py:150
  22.1 24.5 %collective-permute-start.13 = (bf16[256,1024]{1,0:T(8,128)(2,1)S(1)}, bf16[256,1024]{1,0:T(8,128)(2,1)}, u32[]{:S(2)}, u32[]{:S(2)}) collective-permute-start(bf16[256,1024]{1,0:T(8,128)(2,1)S(1)} %bitcast.476), channel_id=1, source_target_pairs={{0,1},{1,0},{2,3},{3,2},{4,5},{5,4},{6,7},{7,6},{8,9},{9,8},{10,11... | collective-permute-start | bytes 1572872 | tf_op jit(solution)/shard_map/ppermute | solution.py:150
  22.1 24.5 %collective-permute-start.2 = (bf16[256,1024]{1,0:T(8,128)(2,1)S(1)}, bf16[256,1024]{1,0:T(8,128)(2,1)}, u32[]{:S(2)}, u32[]{:S(2)}) collective-permute-start(bf16[256,1024]{1,0:T(8,128)(2,1)S(1)} %bitcast.464), channel_id=1, source_target_pairs={{0,1},{1,0},{2,3},{3,2},{4,5},{5,4},{6,7},{7,6},{8,9},{9,8},{10,11... | collective-permute-start | bytes 1572872 | tf_op jit(solution)/shard_map/ppermute | solution.py:150
  23.4 344.4 %reduce-scatter.7.cloned.1.call-start = ((), (), s32[]{:S(2)}) async-start(), calls=%async_computation.10 | async-start | bytes 589824 | tf_op jit(solution)/shard_map/reduce_scatter | solution.py:199
  34.9 11.8 %collective-permute-start.1 = (bf16[256,1024]{1,0:T(8,128)(2,1)}, bf16[256,1024]{1,0:T(8,128)(2,1)S(1)}, u32[]{:S(2)}, u32[]{:S(2)}) collective-permute-start(bf16[256,1024]{1,0:T(8,128)(2,1)} %collective-permute-done), channel_id=1, source_target_pairs={{0,1},{1,0},{2,3},{3,2},{4,5},{5,4},{6,7},{7,6},{8,9},{9,8},{10,11... | collective-permute-start | bytes 1572872 | tf_op jit(solution)/shard_map/ppermute | solution.py:150
  84.7 14.9 %collective-permute-start.3 = (bf16[1024,256]{0,1:T(8,128)(2,1)S(1)}, bf16[1024,256]{0,1:T(8,128)(2,1)S(1)}, u32[]{:S(2)}, u32[]{:S(2)}) collective-permute-start(bf16[1024,256]{0,1:T(8,128)(2,1)S(1)} %bitcast.466), channel_id=1, source_target_pairs={{0,2},{1,3},{2,0},{3,1},{4,6},{5,7},{6,4},{7,5},{8,10},{9,11},{10,... | collective-permute-start | bytes 1572872 | tf_op jit(solution)/shard_map/ppermute | solution.py:150
  87.3 21.5 %collective-permute-start.6 = (bf16[1024,256]{0,1:T(8,128)(2,1)S(1)}, bf16[1024,256]{0,1:T(8,128)(2,1)S(1)}, u32[]{:S(2)}, u32[]{:S(2)}) collective-permute-start(bf16[1024,256]{0,1:T(8,128)(2,1)S(1)} %slice.181), channel_id=1, source_target_pairs={{0,2},{1,3},{2,0},{3,1},{4,6},{5,7},{6,4},{7,5},{8,10},{9,11},{10,... | collective-permute-start | bytes 1572872 | tf_op jit(solution)/shard_map/ppermute | solution.py:150
  87.9 22.5 %collective-permute-start.5 = (bf16[1024,256]{0,1:T(8,128)(2,1)S(1)}, bf16[1024,256]{0,1:T(8,128)(2,1)S(1)}, u32[]{:S(2)}, u32[]{:S(2)}) collective-permute-start(bf16[1024,256]{0,1:T(8,128)(2,1)S(1)} %bitcast.467), channel_id=1, source_target_pairs={{0,1},{1,0},{2,3},{3,2},{4,5},{5,4},{6,7},{7,6},{8,9},{9,8},{10,11... | collective-permute-start | bytes 1572872 | tf_op jit(solution)/shard_map/ppermute | solution.py:150
  99.6 11.0 %collective-permute-start.8 = (bf16[1024,256]{0,1:T(8,128)(2,1)S(1)}, bf16[1024,256]{0,1:T(8,128)(2,1)S(1)}, u32[]{:S(2)}, u32[]{:S(2)}) collective-permute-start(bf16[1024,256]{0,1:T(8,128)(2,1)S(1)} %slice.181), channel_id=1, source_target_pairs={{0,1},{1,0},{2,3},{3,2},{4,5},{5,4},{6,7},{7,6},{8,9},{9,8},{10,11... | collective-permute-start | bytes 1572872 | tf_op jit(solution)/shard_map/ppermute | solution.py:150
  214.1 14.8 %collective-permute-start.15 = (bf16[256,1024]{1,0:T(8,128)(2,1)S(1)}, bf16[256,1024]{1,0:T(8,128)(2,1)S(1)}, u32[]{:S(2)}, u32[]{:S(2)}) collective-permute-start(bf16[256,1024]{1,0:T(8,128)(2,1)S(1)} %fusion.97), channel_id=1, source_target_pairs={{0,2},{1,3},{2,0},{3,1},{4,6},{5,7},{6,4},{7,5},{8,10},{9,11},{10,... | collective-permute-start | bytes 1572872 | tf_op jit(solution)/shard_map/ppermute | solution.py:150
  216.6 23.1 %collective-permute-start.10 = (bf16[256,1024]{1,0:T(8,128)(2,1)S(1)}, bf16[256,1024]{1,0:T(8,128)(2,1)S(1)}, u32[]{:S(2)}, u32[]{:S(2)}) collective-permute-start(bf16[256,1024]{1,0:T(8,128)(2,1)S(1)} %fusion.96), channel_id=1, source_target_pairs={{0,2},{1,3},{2,0},{3,1},{4,6},{5,7},{6,4},{7,5},{8,10},{9,11},{10,... | collective-permute-start | bytes 1572872 | tf_op jit(solution)/shard_map/ppermute | solution.py:150
  241.5 13.8 %collective-permute-start.16 = (bf16[256,1024]{1,0:T(8,128)(2,1)}, bf16[256,1024]{1,0:T(8,128)(2,1)}, u32[]{:S(2)}, u32[]{:S(2)}) collective-permute-start(bf16[256,1024]{1,0:T(8,128)(2,1)} %get-tuple-element.287), channel_id=1, source_target_pairs={{0,2},{1,3},{2,0},{3,1},{4,6},{5,7},{6,4},{7,5},{8,10},{9,11},{10,... | collective-permute-start | bytes 1572872 | tf_op jit(solution)/shard_map/ppermute | solution.py:150
  243.0 15.3 %collective-permute-start.18 = (bf16[256,1024]{1,0:T(8,128)(2,1)}, bf16[256,1024]{1,0:T(8,128)(2,1)}, u32[]{:S(2)}, u32[]{:S(2)}) collective-permute-start(bf16[256,1024]{1,0:T(8,128)(2,1)} %get-tuple-element.287), channel_id=1, source_target_pairs={{0,1},{1,0},{2,3},{3,2},{4,5},{5,4},{6,7},{7,6},{8,9},{9,8},{10,11... | collective-permute-start | bytes 1572872 | tf_op jit(solution)/shard_map/ppermute | solution.py:150
  263.3 126.8 %reduce-scatter.5.cloned.1.call-start = ((), (), s32[]{:S(2)}) async-start(), calls=%async_computation.9 | async-start | bytes 1179648 | tf_op jit(solution)/shard_map/reduce_scatter | solution.py:199
  323.4 138.3 %reduce-scatter.11.cloned.1.call-start = ((), (), s32[]{:S(2)}) async-start(), calls=%async_computation.12 | async-start | bytes 2654208 | tf_op jit(solution)/shard_map/reduce_scatter | solution.py:199
  329.1 230.5 %reduce-scatter.9.cloned.1.call-start = ((), (), s32[]{:S(2)}) async-start(), calls=%async_computation.11 | async-start | bytes 5308416 | tf_op jit(solution)/shard_map/reduce_scatter | solution.py:199
  345.7 11.7 %collective-permute-start.19 = (bf16[2,256,1024]{2,1,0:T(8,128)(2,1)S(1)}, bf16[2,256,1024]{2,1,0:T(8,128)(2,1)}, u32[]{:S(2)}, u32[]{:S(2)}) collective-permute-start(bf16[2,256,1024]{2,1,0:T(8,128)(2,1)S(1)} %fusion.84), channel_id=1, source_target_pairs={{0,1},{1,0},{2,3},{3,2},{4,5},{5,4},{6,7},{7,6},{8,9},{9,8},{10,11... | collective-permute-start | bytes 3145736 | tf_op jit(solution)/shard_map/ppermute | solution.py:150
  361.6 12.6 %collective-permute-start.20 = (bf16[256,1024]{1,0:T(8,128)(2,1)}, bf16[256,1024]{1,0:T(8,128)(2,1)S(1)}, u32[]{:S(2)}, u32[]{:S(2)}) collective-permute-start(bf16[256,1024]{1,0:T(8,128)(2,1)} %fusion.98), channel_id=1, source_target_pairs={{0,2},{1,3},{2,0},{3,1},{4,6},{5,7},{6,4},{7,5},{8,10},{9,11},{10,... | collective-permute-start | bytes 1572872 | tf_op jit(solution)/shard_map/ppermute | solution.py:150
  390.1 73.4 %all-to-all-start = ((bf16[4,32,512]{2,1,0:T(8,128)(2,1)}), bf16[4,32,512]{2,1,0:T(8,128)(2,1)S(1)}, u32[]{:S(2)}, u32[]{:S(2)}) async-start(bf16[4,32,512]{2,1,0:T(8,128)(2,1)} %bitcast.491), calls=%async_computation.1 | async-start | bytes 262144 | tf_op jit(solution)/shard_map/all_to_all | solution.py:381
  559.6 13.2 %all-to-all-start.1 = ((bf16[4,32,2304]{2,1,0:T(8,128)(2,1)}), bf16[4,32,2304]{2,1,0:T(8,128)(2,1)S(1)}, u32[]{:S(2)}, u32[]{:S(2)}) async-start(bf16[4,32,2304]{2,1,0:T(8,128)(2,1)} %bitcast.487), calls=%async_computation.4 | async-start | bytes 1179648 | tf_op jit(solution)/shard_map/all_to_all | solution.py:381
  (63 other events, 376.8 us)
Sparse Core Ops, SparseCore 0:
  11.3 47.9 all-gather.3
  62.0 79.1 all-gather.5
  143.4 50.2 all-gather.7
  263.4 60.6 reduce-scatter.6
  327.8 62.3 reduce-scatter.4
  393.5 68.1 reduce-scatter.10
  465.3 94.2 reduce-scatter.8

commit v2 on v1

--- a/solution.py
+++ b/solution.py
@@ -191,12 +191,81 @@
     return keep + swap(send, 2).astype(F32)
 
 
-def dp_gather(values):
-    return lax.all_gather(values, "dp", axis=0, tiled=True)
-
-
-def dp_scatter(values):
-    return lax.psum_scatter(values.astype(BF), "dp", scatter_dimension=0, tiled=True)
+def after(values, *others):
+    return lax.optimization_barrier((values, others))[0]
+
+
+def ring_length():
+    count = lax.axis_size("dp")
+    return count if count % 2 == 0 and 4 <= count <= 8 else 0
+
+
+def ring_order(count):
+    return list(range(0, count, 2)) + list(range(count - 1, 0, -2))
+
+
+def ring_source(offset):
+    count = lax.axis_size("dp")
+    place = lax.axis_index("dp")
+    spot = jnp.where(place % 2 == 0, place // 2, count - 1 - place // 2)
+    spot = (spot + offset + count) % count
+    return jnp.where(spot < count // 2, 2 * spot, 2 * (count - 1 - spot) + 1)
+
+
+def ring_move(values, step):
+    count = lax.axis_size("dp")
+    order = ring_order(count)
+    return lax.ppermute(
+        values, "dp", [(order[i], order[(i + step) % count]) for i in range(count)]
+    )
+
+
+def dp_gather(shard):
+    count = ring_length()
+    if not count:
+        return (lax.all_gather(shard, "dp", axis=0, tiled=True), shard)
+    rows = shard.shape[0]
+    half = rows // 2
+    whole = jnp.zeros((count * rows, shard.shape[1]), shard.dtype)
+    whole = lax.dynamic_update_slice_in_dim(whole, shard, ring_source(0) * rows, 0)
+    up = down = shard
+    for step in range(1, count // 2):
+        up = ring_move(up, 1)
+        down = ring_move(down, -1)
+        whole = lax.dynamic_update_slice_in_dim(whole, up, ring_source(-step) * rows, 0)
+        whole = lax.dynamic_update_slice_in_dim(whole, down, ring_source(step) * rows, 0)
+    sign = (up, down)
+    first = ring_move(up[:half], 1)
+    second = ring_move(down[half:], -1)
+    start = ring_source(count // 2) * rows
+    whole = lax.dynamic_update_slice_in_dim(whole, first, start, 0)
+    whole = lax.dynamic_update_slice_in_dim(whole, second, start + half, 0)
+    return (whole, sign)
+
+
+def dp_scatter(terms):
+    count = ring_length()
+    if not count:
+        sums = lax.psum_scatter(terms.astype(BF), "dp", scatter_dimension=0, tiled=True)
+        return (sums.astype(F32), sums)
+    rows = terms.shape[0] // count
+    half = rows // 2
+
+    def term(offset):
+        return lax.dynamic_slice_in_dim(terms, ring_source(offset) * rows, rows, 0)
+
+    far = term(count // 2)
+    up = ring_move(far[:half].astype(BF), 1).astype(F32)
+    down = ring_move(far[half:].astype(BF), -1).astype(F32)
+    blank = jnp.zeros((rows - half, terms.shape[1]), F32)
+    up = jnp.concatenate([up, blank])
+    down = jnp.concatenate([jnp.zeros((half, terms.shape[1]), F32), down])
+    sign = (up, down)
+    for step in range(count // 2 - 1, 0, -1):
+        sign = (up, down)
+        up = ring_move((term(step) + up).astype(BF), 1).astype(F32)
+        down = ring_move((term(-step) + down).astype(BF), -1).astype(F32)
+    return (term(0) + up + down, sign)
 
 
 def sum_all(values):
@@ -277,9 +346,9 @@
     gate_up_pack = jnp.concatenate([hidden_columns(gate_weight), hidden_columns(up_weight)], axis=1)
     down_pack = lax.dynamic_slice_in_dim(down_weight, place * piece, piece, 0).astype(BF)
 
-    attention_all = dp_gather(attention_pack)
-    gate_up_all = dp_gather(gate_up_pack)
-    down_all = dp_gather(down_pack)
+    attention_all, sign = dp_gather(attention_pack)
+    gate_up_all, sign = dp_gather(after(gate_up_pack, sign))
+    down_all, sign = dp_gather(after(down_pack, sign))
 
     inputs = seq_gather(tokens[0]).reshape(row_length, width).astype(F32)
     qkv_width = query_here + 2 * key_here
@@ -323,20 +392,25 @@
     ).astype(BF)
     grad_up = (grad_hidden * silu_gate).astype(BF)
     grad_gate_up = jnp.concatenate([grad_gate, grad_up], axis=1)
-    grad_normed = seq_scatter(mm_nt(grad_gate_up, gate_up_all))
-
-    down_sums = dp_scatter(mm_tn(hidden, grad_rows))
-    gate_up_sums = dp_scatter(mm_tn(unit_two, grad_gate_up))
-
+    grad_normed = mm_nt(grad_gate_up, gate_up_all)
+
+    down_terms = mm_tn(hidden, grad_rows)
+    gate_up_terms = mm_tn(unit_two, grad_gate_up)
+    grad_normed, down_terms, gate_up_terms = lax.optimization_barrier(
+        (grad_normed, down_terms, gate_up_terms)
+    )
+    down_sums, sign = dp_scatter(down_terms)
+    gate_up_sums, sign = dp_scatter(after(gate_up_terms, sign))
+
+    grad_normed = seq_scatter(grad_normed)
     after_here = lax.dynamic_slice_in_dim(after_attention, place * local_rows, local_rows, 0)
-    layer_out = (after_here + seq_scatter(mm(hidden, down_all))).astype(BF)
 
     unit_here, factor_here = rms_stats(after_here)
     grad_after = cotangent[0].astype(F32) + rms_back(grad_normed, unit_here, factor_here)
     grad_branch = seq_gather(grad_after.astype(BF)).reshape(row_length, width)
     output_here = lax.dynamic_slice_in_dim(output_all, place * query_here, query_here, 0)
     grad_mixed = mm_nt(grad_branch, output_here).astype(BF)
-    output_sums = dp_scatter(mm_tn(mixed_here, grad_branch))
+    output_terms = mm_tn(mixed_here, grad_branch)
 
     grad_blocks = grad_mixed.reshape(block_count, block_rows, groups_here, group_size, head_dim)
     key_sum, value_sum, query_grad = attention_backward(
@@ -371,15 +445,22 @@
         ],
         axis=1,
     )
-    qkv_sums = dp_scatter(mm_tn(unit_one, qkv_grad))
-    grad_one = seq_scatter(mm_nt(qkv_grad, qkv_weight))
+    qkv_terms = mm_tn(unit_one, qkv_grad)
+    grad_one = mm_nt(qkv_grad, qkv_weight)
+    qkv_terms, grad_one, output_terms = lax.optimization_barrier(
+        (qkv_terms, grad_one, after(output_terms, sign))
+    )
+    output_sums, sign = dp_scatter(output_terms)
+    qkv_sums, sign = dp_scatter(after(qkv_terms, sign))
+    layer_out = (after_here + seq_scatter(mm(after(hidden, qkv_grad), down_all))).astype(BF)
+    grad_one = seq_scatter(grad_one)
     unit_tokens, factor_tokens = rms_stats(tokens[0].astype(F32))
     token_grad = (grad_after + rms_back(grad_one, unit_tokens, factor_tokens)).astype(BF)
     gain_sums = sum_all(gain_terms)
 
     def to_owners(sums):
         return lax.all_to_all(
-            sums.reshape(seq_count, own_rows, -1), "seq", split_axis=0, concat_axis=0, tiled=True
+            sums.astype(BF).reshape(seq_count, own_rows, -1), "seq", split_axis=0, concat_axis=0, tiled=True
         ).astype(F32)
 
     def own(weight):
@@ -411,7 +492,7 @@
         for dp in range(dp_count)
         for seq in range(seq_count)
     ]
-    output_own = lax.ppermute(output_sums, ("dp", "seq"), moves).astype(F32)
+    output_own = lax.ppermute(output_sums.astype(BF), ("dp", "seq"), moves).astype(F32)
 
     return (
         layer_out.reshape(1, local_rows, -1),
@@ -426,7 +507,7 @@
         feed_gain_grad,
         hidden_own[0] * gain_two_own,
         hidden_own[1] * gain_two_own,
-        down_sums.astype(F32),
+        down_sums,
     )
 
 

time: 603 us -> 451 us (0.75)
  waiting for transfers between devices: 345 us -> 110 us
  starting transfers between devices: 26.6 us -> 79.2 us
  local copies, waits for them, and re-layouts: 46 us -> 91.7 us
  matrix products: 100 us -> 84.9 us
  other arithmetic: 59.3 us -> 72.8 us
  between operations: 15.6 us -> 2.32 us
    reduce_scatter x4 -> x0, waiting for transfers between devices: 176 us -> none  [dp_scatter(): lax.psum_scatter(values.astype(BF), 'dp', scatter_dimension=0, tiled=True)]
    all_gather x3 -> x0, waiting for transfers between devices: 71.7 us -> none  [dp_gather(): return lax.all_gather(values, 'dp', axis=0, tiled=True)]
    ppermute x1 -> x57, waiting for transfers between devices: 0.01 us -> 68.7 us  [the longest x56 68.7 us: ring_move(): lax.ppermute(values, 'dp', [(order[i], order[(i + step) % count]) for i i...]
    ppermute x1 -> x57, starting transfers between devices: 1.49 us -> 60 us  [the longest x56 59.4 us: ring_move(): lax.ppermute(values, 'dp', [(order[i], order[(i + step) % count]) for i i...]
    ppermute x21, waiting for transfers between devices: 79.8 us -> 30.8 us  [swap(): return lax.ppermute(values, 'seq', [(i, i ^ bit) for i in range(count)])]
    dynamic_update_slice x0 -> x26, local copies, waits for them, and re-layouts: none -> 43.5 us  [the longest x3 10.9 us: dp_gather(): whole = lax.dynamic_update_slice_in_dim(whole, second, start + half, 0)]
    convert_element_type x3 -> x22, other arithmetic: 2.52 us -> 16.4 us  [the longest x12 8.45 us: dp_scatter(): up = ring_move((term(step) + up).astype(BF), 1).astype(F32)]
    unnamed x105 -> x119, local copies, waits for them, and re-layouts: 19.5 us -> 12.2 us
  transfers between devices with their start and end apart: 36 -> 85, of which waited for: 22 -> 32; matrix products, arithmetic and copies ran while one was open for 26% -> 46% of each run, Pallas kernels for 0% -> 0%
where the time goes in v2:
time: 451 us; the launch traced here: 444 us
  waiting for transfers between devices  110 us (24%)
  local copies, waits for them, and re-layouts  91.7 us (20%)
  matrix products  84.9 us (19%)
  starting transfers between devices  79.2 us (18%)
  other arithmetic  72.8 us (16%)
    ppermute x56, waiting for transfers between devices, ring_move(): lax.ppermute(values, 'dp', [(order[i], order[(i + step) % count]) for i i...  68.7 us
    ppermute x56, starting transfers between devices, ring_move(): lax.ppermute(values, 'dp', [(order[i], order[(i + step) % count]) for i i...  59.4 us
    dot_general x12, matrix products, dot(): lax.dot_general(left, right, (dims, ((), ())), preferred_element_type=F32)  57.1 us
    ppermute x21, waiting for transfers between devices, swap(): return lax.ppermute(values, 'seq', [(i, i ^ bit) for i in range(count)])  30.8 us
    unnamed x119, local copies, waits for them, and re-layouts  12.2 us
    dynamic_update_slice x3, local copies, waits for them, and re-layouts, dp_gather(): whole = lax.dynamic_update_slice_in_dim(whole, second, start + half, 0)  10.9 us
    dynamic_update_slice x9, local copies, waits for them, and re-layouts, dp_gather(): lax.dynamic_update_slice_in_dim(whole, up, ring_source(-step) * rows, 0)  10.2 us
    dynamic_update_slice x9, local copies, waits for them, and re-layouts, dp_gather(): lax.dynamic_update_slice_in_dim(whole, down, ring_source(step) * rows, 0)  10.1 us
  transfers between devices with their start and end apart: 85, of which 32 were waited for; matrix products, arithmetic and copies ran while one was open for 46% of the time, Pallas kernels for 0%

profile of v2, /device:TPU:0, one launch (start us, length us, event | category | flops | bytes accessed | tf_op | source)
XLA Modules:
  0.0 444.1 jit_solution(4061609433357285707)
XLA Ops:
  70.5 19.7 %while.27 = (s32[]{:T(128)}, bf16[2,512,2,2,64]{1,4,3,2,0:T(8,128)(2,1)S(1)}, f32[2,2,2,512]{3,2,1,0:T(2,128)}, s32[2]{0:T(128)S(1)}, s32[1024]{0:T(1024)S(1)}, ...) while((s32[]{:T(128)}, ...), condition=%wide.region_8.9_spmd, body=%wide.region_5.8_spmd.sunk | while | flops 565313024 | bytes 28397788 | solution.py:104
  99.7 5.1 %collective-permute-done.11 = bf16[1024,256]{0,1:T(8,128)(2,1)S(1)} collective-permute-done((bf16[1024,256]{0,1:T(8,128)(2,1)S(1)}, bf16[1024,256]{0,1:T(8,128)(2,1)S(1)}, u32[]{:S(2)}, u32[]{:S(2)}) %collective-permute-start.11) | collective-permute-done | bytes 524320 | tf_op jit(solution)/shard_map/ppermute | solution.py:150
  117.4 6.0 %collective-permute-done.22 = bf16[128,2304]{0,1:T(8,128)(2,1)S(1)} collective-permute-done((bf16[128,2304]{0,1:T(8,128)(2,1)S(1)}, bf16[128,2304]{0,1:T(8,128)(2,1)S(1)}, u32[]{:S(2)}, u32[]{:S(2)}) %collective-permute-start.22) | collective-permute-done | bytes 589856 | tf_op jit(solution)/shard_map/ppermute | solution.py:218
  139.7 6.0 %dynamic_update_slice.108 = bf16[1024,2304]{0,1:T(8,128)(2,1)} dynamic-update-slice(bf16[1024,2304]{0,1:T(8,128)(2,1)} %constant_dynamic-update-slice_fusion.9, bf16[64,2304]{0,1:T(8,128)(2,1)S(1)} %copy.90, s32[]{:T(128)S(6)} %select_n.944, s32[]{:T(128)} %constant.616.clone.1) | dynamic-update-slice | bytes 589828 | tf_op jit(solution)/shard_map/dynamic_update_slice | solution.py:241
  147.0 7.0 %dynamic_update_slice.109 = bf16[1024,2304]{0,1:T(8,128)(2,1)} dynamic-update-slice(bf16[1024,2304]{0,1:T(8,128)(2,1)} %dynamic_update_slice.108, bf16[64,2304]{0,1:T(8,128)(2,1)S(1)} %copy.92, s32[]{:T(128)S(6)} %select_n.945, s32[]{:T(128)} %constant.616.clone.1) | dynamic-update-slice | bytes 589828 | tf_op jit(solution)/shard_map/dynamic_update_slice | solution.py:242
  157.1 8.5 %fusion.114 = f32[1024,2304]{1,0:T(8,128)S(1)} fusion(bf16[1024,2304]{0,1:T(8,128)(2,1)} %dynamic_update_slice.109, f32[1024,1024]{1,0:T(8,128)} %copy-done.14, f32[1024]{0:T(1024)S(1)} %add_rsqrt_fusion.2), kind=kOutput, calls=%fused_computation.347 | convolution fusion | flops 4833935360 | bytes 18354176 | tf_op jit(solution)/shard_map/dot_general | solution.py:16
  179.4 3.7 collective-permute-done.34
  184.4 6.5 %multiply_convert_fusion.1 = (bf16[1024,1152]{1,0:T(8,128)(2,1)S(1)}, bf16[1024,1152]{1,0:T(8,128)(2,1)S(1)}, bf16[1024,1152]{1,0:T(8,128)(2,1)S(1)}) fusion(f32[1024,2304]{1,0:T(8,128)S(1)} %fusion.114, bf16[1024,1024]{1,0:T(8,128)(2,1)S(1)} %bitcast.475, bf16[1152,1024]{1,0:T(8,128)(2,1)} %constant_dynamic-update-slice_fusion), kind=kOutput, calls=%fused_computation.75 | convolution fusion | flops 2433613824 | bytes 20971520 | tf_op jit(solution)/shard_map/dot_general | solution.py:16
  193.6 8.8 %fusion.63 = f32[1024,1024]{1,0:T(8,128)S(1)} fusion(bf16[1024,2304]{0,1:T(8,128)(2,1)} %dynamic_update_slice.109, bf16[1024,1152]{1,0:T(8,128)(2,1)S(1)} %get-tuple-element.343, bf16[1024,1152]{1,0:T(8,128)(2,1)S(1)} %get-tuple-element.342), kind=kOutput, calls=%fused_computation.87 | convolution fusion | flops 4841275392 | bytes 13631488 | tf_op jit(solution)/shard_map/dot_general | solution.py:16
  202.4 7.0 %fusion.62 = f32[1024,2304]{1,0:T(8,128)S(1)} fusion(bf16[1024,1152]{1,0:T(8,128)(2,1)} %copy-done.54, bf16[1024,1152]{1,0:T(8,128)(2,1)S(1)} %get-tuple-element.342, f32[1024,1024]{1,0:T(8,128)S(1)} %copy-done.15, f32[1024]{0:T(1024)S(1)} %add_rsqrt_fusion.2), kind=kOutput, calls=%fused_computation.86 | convolution fusion | flops 4843372544 | bytes 18354176 | tf_op jit(solution)/shard_map/dot_general | solution.py:16
  209.4 8.7 %fusion.123 = f32[1024,1024]{1,0:T(8,128)S(1)} fusion(bf16[1024,1152]{1,0:T(8,128)(2,1)} %copy-done.55, bf16[1152,1024]{1,0:T(8,128)(2,1)} %constant_dynamic-update-slice_fusion), kind=kOutput, calls=%fused_computation.356 | convolution fusion | flops 2415919104 | bytes 8912896 | tf_op jit(solution)/shard_map/dot_general | solution.py:16
  223.5 4.2 collective-permute-done.49
  227.8 6.1 %collective-permute-done.44 = bf16[144,1024]{1,0:T(8,128)(2,1)S(1)} collective-permute-done((bf16[144,1024]{1,0:T(8,128)(2,1)S(1)}, bf16[144,1024]{1,0:T(8,128)(2,1)S(1)}, u32[]{:S(2)}, u32[]{:S(2)}) %collective-permute-start.44) | collective-permute-done | bytes 294944 | tf_op jit(solution)/shard_map/ppermute | solution.py:218
  235.9 5.0 %collective-permute-done.47 = bf16[144,1024]{1,0:T(8,128)(2,1)S(1)} collective-permute-done((bf16[144,1024]{1,0:T(8,128)(2,1)S(1)}, bf16[144,1024]{1,0:T(8,128)(2,1)S(1)}, u32[]{:S(2)}, u32[]{:S(2)}) %collective-permute-start.47) | collective-permute-done | bytes 294944 | tf_op jit(solution)/shard_map/ppermute | solution.py:218
  247.6 5.3 %collective-permute-done.45 = bf16[144,1024]{1,0:T(8,128)(2,1)S(1)} collective-permute-done((bf16[144,1024]{1,0:T(8,128)(2,1)S(1)}, bf16[144,1024]{1,0:T(8,128)(2,1)S(1)}, u32[]{:S(2)}, u32[]{:S(2)}) %collective-permute-start.45) | collective-permute-done | bytes 294944 | tf_op jit(solution)/shard_map/ppermute | solution.py:218
  259.5 9.6 %collective-permute-done.53 = bf16[128,2304]{1,0:T(8,128)(2,1)S(1)} collective-permute-done((bf16[128,2304]{1,0:T(8,128)(2,1)S(1)}, bf16[128,2304]{1,0:T(8,128)(2,1)S(1)}, u32[]{:S(2)}, u32[]{:S(2)}) %collective-permute-start.53) | collective-permute-done | bytes 589856 | tf_op jit(solution)/shard_map/ppermute | solution.py:218
  270.8 9.4 %collective-permute-done.37 = bf16[256,1024]{1,0:T(8,128)(2,1)S(1)} collective-permute-done((bf16[256,1024]{1,0:T(8,128)(2,1)S(1)}, bf16[256,1024]{1,0:T(8,128)(2,1)S(1)}, u32[]{:S(2)}, u32[]{:S(2)}) %collective-permute-start.37) | collective-permute-done | bytes 524320 | tf_op jit(solution)/shard_map/ppermute | solution.py:150
  289.3 5.7 %collective-permute-done.38 = bf16[256,1024]{1,0:T(8,128)(2,1)} collective-permute-done((bf16[256,1024]{1,0:T(8,128)(2,1)}, bf16[256,1024]{1,0:T(8,128)(2,1)}, u32[]{:S(2)}, u32[]{:S(2)}) %collective-permute-start.38) | collective-permute-done | bytes 524320 | tf_op jit(solution)/shard_map/ppermute | solution.py:150
  306.2 29.4 %while.28 = (s32[]{:T(128)}, f32[1024,2,64]{0,2,1:T(8,128)S(1)}, f32[1024,2,64]{0,2,1:T(8,128)}, bf16[2,512,2,2,64]{1,4,3,2,0:T(8,128)(2,1)S(1)}, bf16[2,512,2,2...) while((s32[]{:T(128)}, f32[1024,2,64]{0,2,1:T(8,128)S(1)}, ...), condition=%wide.region_14.15_spmd.clone, body=%wide.region_12.14_spmd.clone.sunk | while | flops 1377697280 | bytes 73478464 | solution.py:140
  346.7 5.4 %fusion.90 = f32[1024,1024]{1,0:T(8,128)} fusion(bf16[1024,768]{0,1:T(8,128)(2,1)} %dynamic_update_slice.100, bf16[1024,128]{0,1:T(8,128)(2,1)S(1)} %bitcast.492, bf16[1024,128]{0,1:T(8,128)(2,1)S(1)} %get-tuple-element.361, bf16[1024,256]{0,1:T(8,128)(2,1)S(1)} %get-tuple-element.355), kind=kOutput, calls=%fused_computation.159 | convolution fusion | flops 1076887552 | bytes 6291456 | tf_op jit(solution)/shard_map/dot_general | solution.py:16
  365.1 3.8 collective-permute-done.75
  374.0 3.5 all-to-all-start.1
  414.3 4.2 all-to-all-start
  431.0 10.6 %collective-permute-done.56 = bf16[256,1024]{1,0:T(8,128)(2,1)S(1)} collective-permute-done((bf16[256,1024]{1,0:T(8,128)(2,1)S(1)}, bf16[256,1024]{1,0:T(8,128)(2,1)S(1)}, u32[]{:S(2)}, u32[]{:S(2)}) %collective-permute-start.56) | collective-permute-done | bytes 524320 | tf_op jit(solution)/shard_map/ppermute | solution.py:150
  (511 shorter events, 298.9 us)
Async XLA Ops:
  0.7 55.7 %collective-permute-start.2 = (bf16[256,1024]{1,0:T(8,128)(2,1)}, bf16[256,1024]{1,0:T(8,128)(2,1)}, u32[]{:S(2)}, u32[]{:S(2)}) collective-permute-start(bf16[256,1024]{1,0:T(8,128)(2,1)} %bitcast.467), channel_id=1, source_target_pairs={{0,1},{1,0},{2,3},{3,2},{4,5},{5,4},{6,7},{7,6},{8,9},{9,8},{10,11... | collective-permute-start | bytes 1572872 | tf_op jit(solution)/shard_map/ppermute | solution.py:150
  1.2 31.2 %collective-permute-start = (bf16[256,1024]{1,0:T(8,128)(2,1)}, bf16[256,1024]{1,0:T(8,128)(2,1)}, u32[]{:S(2)}, u32[]{:S(2)}) collective-permute-start(bf16[256,1024]{1,0:T(8,128)(2,1)} %bitcast.468), channel_id=1, source_target_pairs={{0,2},{1,3},{2,0},{3,1},{4,6},{5,7},{6,4},{7,5},{8,10},{9,11},{10,... | collective-permute-start | bytes 1572872 | tf_op jit(solution)/shard_map/ppermute | solution.py:150
  11.0 21.3 %collective-permute-start.25 = (bf16[256,1024]{1,0:T(8,128)(2,1)S(1)}, bf16[256,1024]{1,0:T(8,128)(2,1)}, u32[]{:S(2)}, u32[]{:S(2)}) collective-permute-start(bf16[256,1024]{1,0:T(8,128)(2,1)S(1)} %bitcast.478), channel_id=1, source_target_pairs={{0,2},{1,3},{2,0},{3,1},{4,6},{5,7},{6,4},{7,5},{8,10},{9,11},{10,... | collective-permute-start | bytes 1572872 | tf_op jit(solution)/shard_map/ppermute | solution.py:150
  32.4 26.4 %collective-permute-start.27 = (bf16[256,1024]{1,0:T(8,128)(2,1)S(1)}, bf16[256,1024]{1,0:T(8,128)(2,1)S(1)}, u32[]{:S(2)}, u32[]{:S(2)}) collective-permute-start(bf16[256,1024]{1,0:T(8,128)(2,1)S(1)} %bitcast.479), channel_id=1, source_target_pairs={{0,1},{1,0},{2,3},{3,2},{4,5},{5,4},{6,7},{7,6},{8,9},{9,8},{10,11... | collective-permute-start | bytes 1572872 | tf_op jit(solution)/shard_map/ppermute | solution.py:150
  32.4 26.4 %collective-permute-start.1 = (bf16[256,1024]{1,0:T(8,128)(2,1)}, bf16[256,1024]{1,0:T(8,128)(2,1)S(1)}, u32[]{:S(2)}, u32[]{:S(2)}) collective-permute-start(bf16[256,1024]{1,0:T(8,128)(2,1)} %collective-permute-done), channel_id=1, source_target_pairs={{0,1},{1,0},{2,3},{3,2},{4,5},{5,4},{6,7},{7,6},{8,9},{9,8},{10,11... | collective-permute-start | bytes 1572872 | tf_op jit(solution)/shard_map/ppermute | solution.py:150
  34.6 25.7 %collective-permute-start.26 = (bf16[256,1024]{1,0:T(8,128)(2,1)}, bf16[256,1024]{1,0:T(8,128)(2,1)S(1)}, u32[]{:S(2)}, u32[]{:S(2)}) collective-permute-start(bf16[256,1024]{1,0:T(8,128)(2,1)} %collective-permute-done.25), channel_id=1, source_target_pairs={{0,1},{1,0},{2,3},{3,2},{4,5},{5,4},{6,7},{7,6},{8,9},{9,8},{10,11... | collective-permute-start | bytes 1572872 | tf_op jit(solution)/shard_map/ppermute | solution.py:150
  50.9 42.3 %collective-permute-start.18 = (bf16[128,2304]{0,1:T(8,128)(2,1)}, bf16[128,2304]{0,1:T(8,128)(2,1)}, u32[]{:S(2)}, u32[]{:S(2)}) collective-permute-start(bf16[128,2304]{0,1:T(8,128)(2,1)} %pad_maximum_fusion.9), channel_id=1, source_target_pairs={{0,4},{8,0},{16,8},{24,16},{28,24},{20,28},{12,20},{4,12},{1,5},{9... | collective-permute-start | bytes 1769480 | tf_op jit(solution)/shard_map/ppermute | solution.py:218
  56.4 36.7 %collective-permute-start.17 = (bf16[128,2304]{0,1:T(8,128)(2,1)}, bf16[128,2304]{0,1:T(8,128)(2,1)}, u32[]{:S(2)}, u32[]{:S(2)}) collective-permute-start(bf16[128,2304]{0,1:T(8,128)(2,1)} %pad_maximum_fusion.9), channel_id=1, source_target_pairs={{0,8},{8,16},{16,24},{24,28},{28,20},{20,12},{12,4},{4,0},{1,9},{9... | collective-permute-start | bytes 1769480 | tf_op jit(solution)/shard_map/ppermute | solution.py:218
  58.7 40.5 %collective-permute-start.16 = (bf16[1024,256]{0,1:T(8,128)(2,1)}, bf16[1024,256]{0,1:T(8,128)(2,1)}, u32[]{:S(2)}, u32[]{:S(2)}) collective-permute-start(bf16[1024,256]{0,1:T(8,128)(2,1)} %slice.247), channel_id=1, source_target_pairs={{0,1},{1,0},{2,3},{3,2},{4,5},{5,4},{6,7},{7,6},{8,9},{9,8},{10,11... | collective-permute-start | bytes 1572872 | tf_op jit(solution)/shard_map/ppermute | solution.py:150
  58.8 36.4 %collective-permute-start.14 = (bf16[1024,256]{0,1:T(8,128)(2,1)}, bf16[1024,256]{0,1:T(8,128)(2,1)}, u32[]{:S(2)}, u32[]{:S(2)}) collective-permute-start(bf16[1024,256]{0,1:T(8,128)(2,1)} %slice.247), channel_id=1, source_target_pairs={{0,2},{1,3},{2,0},{3,1},{4,6},{5,7},{6,4},{7,5},{8,10},{9,11},{10,... | collective-permute-start | bytes 1572872 | tf_op jit(solution)/shard_map/ppermute | solution.py:150
  124.0 30.0 %collective-permute-start.29 = (bf16[144,1024]{1,0:T(8,128)(2,1)S(1)}, bf16[144,1024]{1,0:T(8,128)(2,1)}, u32[]{:S(2)}, u32[]{:S(2)}) collective-permute-start(bf16[144,1024]{1,0:T(8,128)(2,1)S(1)} %copy-done.35), channel_id=1, source_target_pairs={{0,4},{8,0},{16,8},{24,16},{28,24},{20,28},{12,20},{4,12},{1,5},{9... | collective-permute-start | bytes 884744 | tf_op jit(solution)/shard_map/ppermute | solution.py:218
  125.3 31.8 %collective-permute-start.28 = (bf16[144,1024]{1,0:T(8,128)(2,1)S(1)}, bf16[144,1024]{1,0:T(8,128)(2,1)}, u32[]{:S(2)}, u32[]{:S(2)}) collective-permute-start(bf16[144,1024]{1,0:T(8,128)(2,1)S(1)} %copy-done.35), channel_id=1, source_target_pairs={{0,8},{8,16},{16,24},{24,28},{28,20},{20,12},{12,4},{4,0},{1,9},{9... | collective-permute-start | bytes 884744 | tf_op jit(solution)/shard_map/ppermute | solution.py:218
  220.1 35.7 %collective-permute-start.41 = (bf16[2,256,1024]{2,1,0:T(8,128)(2,1)S(1)}, bf16[2,256,1024]{2,1,0:T(8,128)(2,1)S(1)}, u32[]{:S(2)}, u32[]{:S(2)}) collective-permute-start(bf16[2,256,1024]{2,1,0:T(8,128)(2,1)S(1)} %fusion.84), channel_id=1, source_target_pairs={{0,1},{1,0},{2,3},{3,2},{4,5},{5,4},{6,7},{7,6},{8,9},{9,8},{10,11... | collective-permute-start | bytes 3145736 | tf_op jit(solution)/shard_map/ppermute | solution.py:150
  235.8 22.2 %collective-permute-start.36 = (bf16[2,256,1024]{2,1,0:T(8,128)(2,1)S(1)}, bf16[2,256,1024]{2,1,0:T(8,128)(2,1)S(1)}, u32[]{:S(2)}, u32[]{:S(2)}) collective-permute-start(bf16[2,256,1024]{2,1,0:T(8,128)(2,1)S(1)} %fusion.83), channel_id=1, source_target_pairs={{0,1},{1,0},{2,3},{3,2},{4,5},{5,4},{6,7},{7,6},{8,9},{9,8},{10,11... | collective-permute-start | bytes 3145736 | tf_op jit(solution)/shard_map/ppermute | solution.py:150
  247.6 47.4 %collective-permute-start.51 = (bf16[128,2304]{1,0:T(8,128)(2,1)}, bf16[128,2304]{1,0:T(8,128)(2,1)}, u32[]{:S(2)}, u32[]{:S(2)}) collective-permute-start(bf16[128,2304]{1,0:T(8,128)(2,1)} %get-tuple-element.346), channel_id=1, source_target_pairs={{0,8},{8,16},{16,24},{24,28},{28,20},{20,12},{12,4},{4,0},{1,9},{9... | collective-permute-start | bytes 1769480 | tf_op jit(solution)/shard_map/ppermute | solution.py:218
  255.3 31.8 %collective-permute-start.81 = (bf16[144,1024]{1,0:T(8,128)(2,1)}, bf16[144,1024]{1,0:T(8,128)(2,1)}, u32[]{:S(2)}, u32[]{:S(2)}) collective-permute-start(bf16[144,1024]{1,0:T(8,128)(2,1)} %get-tuple-element.349), channel_id=1, source_target_pairs={{0,8},{8,16},{16,24},{24,28},{28,20},{20,12},{12,4},{4,0},{1,9},{9... | collective-permute-start | bytes 884744 | tf_op jit(solution)/shard_map/ppermute | solution.py:218
  255.8 31.3 %collective-permute-start.82 = (bf16[144,1024]{1,0:T(8,128)(2,1)S(1)}, bf16[144,1024]{1,0:T(8,128)(2,1)}, u32[]{:S(2)}, u32[]{:S(2)}) collective-permute-start(bf16[144,1024]{1,0:T(8,128)(2,1)S(1)} %get-tuple-element.350), channel_id=1, source_target_pairs={{0,4},{8,0},{16,8},{24,16},{28,24},{20,28},{12,20},{4,12},{1,5},{9... | collective-permute-start | bytes 884744 | tf_op jit(solution)/shard_map/ppermute | solution.py:218
  258.0 24.7 %collective-permute-start.42 = (bf16[256,1024]{1,0:T(8,128)(2,1)S(1)}, bf16[256,1024]{1,0:T(8,128)(2,1)S(1)}, u32[]{:S(2)}, u32[]{:S(2)}) collective-permute-start(bf16[256,1024]{1,0:T(8,128)(2,1)S(1)} %fusion.98), channel_id=1, source_target_pairs={{0,2},{1,3},{2,0},{3,1},{4,6},{5,7},{6,4},{7,5},{8,10},{9,11},{10,... | collective-permute-start | bytes 1572872 | tf_op jit(solution)/shard_map/ppermute | solution.py:150
  298.2 72.8 %collective-permute-start.79 = (bf16[128,2304]{1,0:T(8,128)(2,1)}, bf16[128,2304]{1,0:T(8,128)(2,1)}, u32[]{:S(2)}, u32[]{:S(2)}) collective-permute-start(bf16[128,2304]{1,0:T(8,128)(2,1)} %get-tuple-element.344), channel_id=1, source_target_pairs={{0,8},{8,16},{16,24},{24,28},{28,20},{20,12},{12,4},{4,0},{1,9},{9... | collective-permute-start | bytes 1769480 | tf_op jit(solution)/shard_map/ppermute | solution.py:218
  298.4 72.7 %collective-permute-start.80 = (bf16[128,2304]{1,0:T(8,128)(2,1)}, bf16[128,2304]{1,0:T(8,128)(2,1)}, u32[]{:S(2)}, u32[]{:S(2)}) collective-permute-start(bf16[128,2304]{1,0:T(8,128)(2,1)} %get-tuple-element.345), channel_id=1, source_target_pairs={{0,4},{8,0},{16,8},{24,16},{28,24},{20,28},{12,20},{4,12},{1,5},{9... | collective-permute-start | bytes 1769480 | tf_op jit(solution)/shard_map/ppermute | solution.py:218
  354.5 23.0 %collective-permute-start.60 = (bf16[16,1024]{1,0:T(8,128)(2,1)S(1)}, bf16[16,1024]{1,0:T(8,128)(2,1)S(1)}, u32[]{:S(2)}, u32[]{:S(2)}) collective-permute-start(bf16[16,1024]{1,0:T(8,128)(2,1)S(1)} %get-tuple-element.415), channel_id=1, source_target_pairs={{0,4},{8,0},{16,8},{24,16},{28,24},{20,28},{12,20},{4,12},{1,5},{9... | collective-permute-start | bytes 98312 | tf_op jit(solution)/shard_map/ppermute | solution.py:218
  369.1 21.0 %collective-permute-start.67 = (bf16[64,512]{1,0:T(8,128)(2,1)S(1)}, bf16[64,512]{1,0:T(8,128)(2,1)S(1)}, u32[]{:S(2)}, u32[]{:S(2)}) collective-permute-start(bf16[64,512]{1,0:T(8,128)(2,1)S(1)} %get-tuple-element.413), channel_id=1, source_target_pairs={{0,4},{8,0},{16,8},{24,16},{28,24},{20,28},{12,20},{4,12},{1,5},{9... | collective-permute-start | bytes 196616 | tf_op jit(solution)/shard_map/ppermute | solution.py:218
  371.0 54.0 %collective-permute-start.55 = (bf16[2,256,1024]{2,1,0:T(8,128)(2,1)}, bf16[2,256,1024]{2,1,0:T(8,128)(2,1)}, u32[]{:S(2)}, u32[]{:S(2)}) collective-permute-start(bf16[2,256,1024]{2,1,0:T(8,128)(2,1)} %fusion.85), channel_id=1, source_target_pairs={{0,1},{1,0},{2,3},{3,2},{4,5},{5,4},{6,7},{7,6},{8,9},{9,8},{10,11... | collective-permute-start | bytes 3145736 | tf_op jit(solution)/shard_map/ppermute | solution.py:150
  374.0 29.1 %all-to-all-start.1 = ((bf16[4,32,2304]{2,1,0:T(8,128)(2,1)}), bf16[4,32,2304]{2,1,0:T(8,128)(2,1)S(1)}, u32[]{:S(2)}, u32[]{:S(2)}) async-start(bf16[4,32,2304]{2,1,0:T(8,128)(2,1)} %bitcast.70), calls=%async_computation.1 | async-start | bytes 1179648 | tf_op jit(solution)/shard_map/all_to_all | solution.py:462
  (119 other events, 1050.3 us)
